TPU v7x, 32 devices: a whole 2x2x4 slice. The times are simulated.
32 devices in a mesh: dp: 4 (over y, x), seq: 2 (over core), tensor: 4 (over z).
Axes of the slice: x: 2, y: 2, z: 4, core: 2. Of those that a mesh axis runs over, the one named last changes fastest.
Arguments:
- entry_x: bfloat16 [48, 512, 1024], P('dp', 'seq', 'tensor'), may hold values from -6 to 6
- entry_z: bfloat16 [48, 512, 1024], P('dp', 'seq', 'tensor'), may hold values from -6 to 6
- entry_bc: bfloat16 [48, 512, 256], P('dp', 'seq'), may hold values from -6 to 6
- entry_dt: bfloat16 [48, 512, 16], P('dp', 'seq', 'tensor'), may hold values from -3 to 3
- source_rank: int32 [4, 4], replicated, may hold values from 0 to 3, as said below
- source_slot: int32 [4, 4], replicated, may hold values from 0 to 11, as said below
- row_spans: int32 [4, 4], replicated, may hold values from 0 to 4, as said below
- conv_x_weight: float32 [4, 1024], P(None, 'tensor'), may hold values from -3 to 3
- conv_x_bias: float32 [1024], P('tensor'), may hold values from -2 to 2
- conv_bc_weight: float32 [4, 256], replicated, may hold values from -3 to 3
- conv_bc_bias: float32 [256], replicated, may hold values from -2 to 2
- dt_bias: float32 [16], P('tensor'), may hold values from -0.5 to 0.5
- a_log: float32 [16], P('tensor')
- d_skip: float32 [16], P('tensor'), may hold values from 0.5 to 1.5
- norm_gain: float32 [1024], P('tensor'), may hold values from 0.1 to 1.9
- out_weight: bfloat16 [1024, 4096], P('tensor'), may hold values from -0.1875 to 0.1875
Outputs:
- mixed: bfloat16 [16, 512, 4096], P('dp', 'seq', 'tensor')
Inputs may be any that keep to these rules, and one draw needn't show every extreme that they name: `source_rank`: each slot's block is held on entry by its own data rank or by a data rank next to it; no entry slot serves two slots. `source_slot`: together with source_rank: an entry slot of the named data rank. `row_spans`: on every data rank the nonzero lengths come first and sum to 4.
All inputs are finite; a program needn't handle non-finite values.
Results may differ from a plain program's by a relative error of at most 0.0095.
Values may be sent and summed in bfloat16 or wider, within the bound.
A program may use at most 128 MiB of HBM per device.

v0:
```python
import functools

import jax
import jax.numpy as jnp
from jax import lax
from jax.experimental import pallas as pl
from jax.experimental.pallas import tpu as pltpu
from jax.sharding import PartitionSpec as P

HEAD = 64
EXTRA = 16
EPS = 1e-05
F32 = jnp.float32
BF16 = jnp.bfloat16
HIGHEST = lax.Precision.HIGHEST


def shifted(value, axis, steps):
    count = lax.axis_size(axis)
    first, last = (max(0, -steps), min(count, count - steps))
    return lax.ppermute(value, axis, [(source, source + steps) for source in range(first, last)])


def pack_kernel(slot_ref, peer_ref, x_ref, z_ref, bc_ref, dt_ref, tail_ref, main_ref, gate_ref):
    length, width = x_ref.shape[1:]
    heads = dt_ref.shape[1]
    main_ref[0, :length, :width] = x_ref[0]
    main_ref[0, :length, width:] = bc_ref[0]
    main_ref[0, length:, :] = tail_ref[0]
    main_ref[0, length : length + heads, : dt_ref.shape[2]] = dt_ref[0]
    gate_ref[0] = z_ref[0]


def pack(source_slot, peer, entry_x, entry_z, entry_bc, dt_rows, tails):
    count = source_slot.shape[1]
    length, width = entry_x.shape[1:]
    full = width + entry_bc.shape[2]

    def spec(array):
        return pl.BlockSpec((1,) + array.shape[1:], lambda j, slots, who: (slots[who[0], j], 0, 0))

    def out(rows, cols):
        return pl.BlockSpec((1, rows, cols), lambda j, slots, who: (j, 0, 0))

    operands = (entry_x, entry_z, entry_bc, dt_rows, tails)
    return pl.pallas_call(
        pack_kernel,
        grid_spec=pltpu.PrefetchScalarGridSpec(
            num_scalar_prefetch=2,
            grid=(count,),
            in_specs=[spec(array) for array in operands],
            out_specs=[out(length + EXTRA, full), out(length, width)],
        ),
        out_shape=[
            jax.ShapeDtypeStruct((count, length + EXTRA, full), BF16),
            jax.ShapeDtypeStruct((count, length, width), BF16),
        ],
        cost_estimate=pl.CostEstimate(flops=0, bytes_accessed=4_000_000, transcendentals=0),
        name="pack",
    )(source_slot, peer, *operands)


def slot_row(spans_ref, rank, j, count):
    start, opens, final = jnp.int32(0), jnp.int32(0), jnp.int32(0)
    for k in range(count):
        span = spans_ref[rank, k]
        inside = (j >= start) & (j < start + span)
        opens = jnp.where(inside & (j == start), 1, opens)
        final = jnp.where(inside, start + span - 1, final)
        start = start + span
    return opens == 1, final


def choose(rank_of, rank, own, left, right):
    return jnp.where(rank_of == rank, own, jnp.where(rank_of < rank, left, right))


def scan_kernel(
    rank_ref, source_ref, spans_ref, dtb_ref, alog_ref, skip_ref,
    own_ref, left_ref, right_ref, wx_ref, wbc_ref, bx_ref, bbc_ref,
    base_ref, scale_ref, c_ref, end_ref,
    joined, tail, state, decay, mixes, spread, weighted,
):
    j = pl.program_id(0)
    rank = rank_ref[0]
    count = own_ref.shape[0]
    length = own_ref.shape[1] - EXTRA
    width = wx_ref.shape[1]
    bc_width = wbc_ref.shape[1]
    states = bc_width // 2
    taps = wx_ref.shape[0]
    heads = width // HEAD
    opens, final = slot_row(spans_ref, rank, j, count)

    def moved(slot, rows):
        parts = [ref[slot, rows, :].astype(F32) for ref in (own_ref, left_ref, right_ref)]
        return choose(source_ref[rank, slot], rank, *parts)

    before = moved(final, slice(length, length + EXTRA))[EXTRA - 8 :]
    joined[0:8, :] = jnp.where(opens, before, tail[...])
    joined[8 : 8 + length, :] = moved(j, slice(0, length))
    steps = moved(j, slice(length, length + EXTRA))[0:8, :length]
    tail[...] = joined[length : length + 8, :]

    def conv(weight_ref, bias_ref, first, last):
        total = bias_ref[...]
        for k in range(taps):
            offset = 8 - (taps - 1) + k
            total = total + weight_ref[k : k + 1, :] * joined[offset : offset + length, first:last]
        return (total / (1.0 + jnp.exp(-total))).astype(BF16)

    xc = conv(wx_ref, bx_ref, 0, width)
    bc = conv(wbc_ref, bbc_ref, width, width + bc_width)
    b_rows = jnp.transpose(bc[:, :states].astype(F32))
    c_act = bc[:, states:]
    c_ref[0] = c_act

    row = lax.broadcasted_iota(jnp.int32, (8, length), 0)
    shift = jnp.zeros((8, length), F32)
    rate = jnp.zeros((8, length), F32)
    for h in range(heads):
        shift = jnp.where(row == h, dtb_ref[h], shift)
        rate = jnp.where(row == h, alog_ref[h], rate)
    raw = steps + shift
    dt = jnp.maximum(raw, 0.0) + jnp.log1p(jnp.exp(-jnp.abs(raw)))
    rates = jnp.where(row < heads, -jnp.exp(rate) * dt, 0.0)
    t_at = lax.broadcasted_iota(jnp.int32, (length, length), 0)
    s_at = lax.broadcasted_iota(jnp.int32, (length, length), 1)
    lower = t_at >= s_at
    ones = jnp.where(lower, 1.0, 0.0).astype(BF16)
    hi = rates.astype(BF16)
    mid = (rates - hi.astype(F32)).astype(BF16)
    low = (rates - hi.astype(F32) - mid.astype(F32)).astype(BF16)
    across = (((1,), (1,)), ((), ()))
    cum_rows = sum(
        lax.dot_general(part, ones, across, preferred_element_type=F32) for part in (low, mid, hi)
    )
    padded = jnp.concatenate([cum_rows] + [jnp.zeros((120, length), F32)], 0)
    cum_cols = jnp.transpose(padded)
    total = cum_rows[:, length - 1 :]
    gone = jnp.exp(total - cum_rows) * dt

    gram = jnp.dot(c_act, b_rows.astype(BF16), preferred_element_type=F32)
    lane_head = lax.broadcasted_iota(jnp.int32, (length, width), 1) // HEAD
    cum_wide = jnp.zeros((length, width), F32)
    skip_wide = jnp.zeros((1, width), F32)
    for h in range(heads):
        column = cum_cols[:, h : h + 1]
        gap = jnp.where(lower, column - cum_rows[h : h + 1, :], -jnp.inf)
        mix = gram * jnp.exp(gap) * dt[h : h + 1, :]
        mixes[:, h * length : (h + 1) * length] = mix.astype(BF16)
        weighted[:, h * length : (h + 1) * length] = (gone[h : h + 1, :] * b_rows).astype(BF16)
        spread[h * length : (h + 1) * length, :] = jnp.where(
            lane_head == h, xc.astype(F32), 0.0
        ).astype(BF16)
        cum_wide = jnp.where(lane_head == h, column, cum_wide)
        skip_wide = jnp.where(lane_head[0:1] == h, skip_ref[h], skip_wide)
    intra = jnp.dot(mixes[...], spread[...], preferred_element_type=F32)
    contrib = jnp.dot(weighted[...], spread[...], preferred_element_type=F32)

    grown = jnp.exp(cum_wide)
    block_decay = grown[length - 1 : length, :]
    entering = jnp.where(opens, 0.0, state[...])
    passed = jnp.where(opens, 1.0, decay[...])
    ent_hi = entering.astype(BF16)
    ent_lo = (entering - ent_hi.astype(F32)).astype(BF16)
    read = jnp.dot(c_act, ent_hi, preferred_element_type=F32) + jnp.dot(
        c_act, ent_lo, preferred_element_type=F32
    )
    base_ref[0] = intra + grown * read + skip_wide * xc.astype(F32)
    scale_ref[0] = grown * passed
    ended = block_decay * entering + contrib
    state[...] = ended
    decay[...] = passed * block_decay
    end_ref[0] = ended


def scan(rank, source_rank, row_spans, dt_bias, a_log, d_skip, own, left, right, wx, wbc, bx, bbc):
    count, tall, full = own.shape
    length = tall - EXTRA
    width, bc_width = wx.shape[1], wbc.shape[1]
    heads, states = width // HEAD, bc_width // 2

    def whole(array):
        return pl.BlockSpec(array.shape, lambda j, *_: (0,) * array.ndim)

    def slot(rows, cols):
        return pl.BlockSpec((1, rows, cols), lambda j, *_: (j, 0, 0))

    return pl.pallas_call(
        scan_kernel,
        grid_spec=pltpu.PrefetchScalarGridSpec(
            num_scalar_prefetch=6,
            grid=(count,),
            in_specs=[whole(array) for array in (own, left, right, wx, wbc, bx, bbc)],
            out_specs=[
                slot(length, width), slot(length, width), slot(length, states), slot(states, width)
            ],
            scratch_shapes=[
                pltpu.VMEM((length + 8, full), F32),
                pltpu.VMEM((8, full), F32),
                pltpu.VMEM((states, width), F32),
                pltpu.VMEM((1, width), F32),
                pltpu.VMEM((length, heads * length), BF16),
                pltpu.VMEM((heads * length, width), BF16),
                pltpu.VMEM((states, heads * length), BF16),
            ],
        ),
        out_shape=[
            jax.ShapeDtypeStruct((count, length, width), F32),
            jax.ShapeDtypeStruct((count, length, width), F32),
            jax.ShapeDtypeStruct((count, length, states), BF16),
            jax.ShapeDtypeStruct((count, states, width), F32),
        ],
        compiler_params=pltpu.CompilerParams(vmem_limit_bytes=40 << 20),
        cost_estimate=pl.CostEstimate(
            flops=3_000_000_000, bytes_accessed=8_000_000, transcendentals=2_000_000
        ),
        name="scan",
    )(rank, source_rank, row_spans, dt_bias, a_log, d_skip, own, left, right, wx, wbc, bx, bbc)


def gate_kernel(
    rank_ref, source_ref, spans_ref,
    base_ref, scale_ref, c_ref, carried_ref, own_ref, left_ref, right_ref, gain_ref, out_ref,
):
    j = pl.program_id(0)
    rank = rank_ref[0]
    _, final = slot_row(spans_ref, rank, j, carried_ref.shape[0])
    carried = carried_ref[final]
    high = carried.astype(BF16)
    low = (carried - high.astype(F32)).astype(BF16)
    c_act = c_ref[0]
    read = jnp.dot(c_act, high, preferred_element_type=F32) + jnp.dot(
        c_act, low, preferred_element_type=F32
    )
    y = base_ref[0] + scale_ref[0] * read
    parts = [ref[0].astype(F32) for ref in (own_ref, left_ref, right_ref)]
    z = choose(source_ref[rank, j], rank, *parts)
    g = y * (z / (1.0 + jnp.exp(-z)))
    inverse = lax.rsqrt(jnp.mean(g * g, axis=-1, keepdims=True) + EPS)
    out_ref[0] = (g * inverse * gain_ref[...]).astype(BF16)


def gate(rank, source_rank, row_spans, base, scale, c_act, carried, own, left, right, gain):
    count, length, width = base.shape

    def whole(array):
        return pl.BlockSpec(array.shape, lambda j, *_: (0,) * array.ndim)

    def slot(array):
        return pl.BlockSpec((1,) + array.shape[1:], lambda j, *_: (j, 0, 0))

    return pl.pallas_call(
        gate_kernel,
        grid_spec=pltpu.PrefetchScalarGridSpec(
            num_scalar_prefetch=3,
            grid=(count,),
            in_specs=[slot(base), slot(scale), slot(c_act), whole(carried)]
            + [slot(own)] * 3
            + [whole(gain)],
            out_specs=slot(base),
        ),
        out_shape=jax.ShapeDtypeStruct((count, length, width), BF16),
        name="gate",
    )(rank, source_rank, row_spans, base, scale, c_act, carried, own, left, right, gain)


def project_kernel(rows_ref, weight_ref, out_ref):
    total = jnp.dot(rows_ref[0, 0], weight_ref[0], preferred_element_type=F32)
    for i in range(1, weight_ref.shape[0]):
        total = total + jnp.dot(rows_ref[i, 0], weight_ref[i], preferred_element_type=F32)
    out_ref[0] = total.astype(BF16)


def project(rows, weight):
    groups, count, length, width = rows.shape
    cols = weight.shape[2]
    return pl.pallas_call(
        project_kernel,
        grid=(count,),
        in_specs=[
            pl.BlockSpec((groups, 1, length, width), lambda j: (0, j, 0, 0)),
            pl.BlockSpec(weight.shape, lambda j: (0, 0, 0)),
        ],
        out_specs=pl.BlockSpec((1, length, cols), lambda j: (j, 0, 0)),
        out_shape=jax.ShapeDtypeStruct((count, length, cols), BF16),
        compiler_params=pltpu.CompilerParams(vmem_limit_bytes=40 << 20),
        name="project",
    )(rows, weight)


def body(
    entry_x, entry_z, entry_bc, entry_dt, source_rank, source_slot, row_spans,
    conv_x_weight, conv_x_bias, conv_bc_weight, conv_bc_bias,
    dt_bias, a_log, d_skip, norm_gain, out_weight,
):
    length, width = entry_x.shape[1:]
    ranks, groups = lax.axis_size("dp"), lax.axis_size("tensor")
    me = lax.axis_index("dp").astype(jnp.int32)
    rank = me.reshape(1)

    dt_rows = jnp.swapaxes(entry_dt, 1, 2)
    ends = jnp.concatenate([entry_x[:, length - EXTRA :], entry_bc[:, length - EXTRA :]], 2)
    tails = shifted(ends, "seq", 1)

    def packed(peer):
        peer = jnp.clip(peer, 0, ranks - 1).astype(jnp.int32)
        return pack(source_slot, peer, entry_x, entry_z, entry_bc, dt_rows, tails)

    down_main, down_gate = packed(rank - 1)
    up_main, up_gate = packed(rank + 1)
    right = shifted(down_main, "dp", -1)
    left = shifted(up_main, "dp", 1)
    own, own_gate = packed(rank)

    cols = out_weight.shape[1] // groups
    pieces = jnp.swapaxes(out_weight.reshape(width, groups, cols), 0, 1)
    weight = lax.all_to_all(pieces, "tensor", 0, 0, tiled=True)

    down_gate, up_gate, left, right = lax.optimization_barrier((down_gate, up_gate, left, right))
    right_gate = shifted(down_gate, "dp", -1)
    left_gate = shifted(up_gate, "dp", 1)

    base, scale, c_act, ended = scan(
        rank, source_rank, row_spans, dt_bias, a_log, d_skip, own, left, right,
        conv_x_weight, conv_bc_weight, conv_x_bias.reshape(1, -1), conv_bc_bias.reshape(1, -1),
    )
    carried = shifted(ended, "seq", 1)
    normed = gate(
        rank, source_rank, row_spans, base, scale, c_act, carried,
        own_gate, left_gate, right_gate, norm_gain.reshape(1, -1),
    )
    gathered = lax.all_gather(normed, "tensor", axis=0)
    return project(gathered, weight)


def solution(mesh):
    split = P("dp", "seq", "tensor")
    placed = (
        split, split, P("dp", "seq", None), split, P(), P(), P(),
        P(None, "tensor"), P("tensor"), P(), P(),
        P("tensor"), P("tensor"), P("tensor"), P("tensor"), P("tensor", None),
    )
    return jax.shard_map(body, mesh=mesh, in_specs=placed, out_specs=split, check_vma=False)
```

profile of v0, /device:TPU:0, one launch (start us, length us, event | category | flops | bytes accessed | tf_op | source)
XLA Modules:
  0.0 192.8 jit_solution(11157662002556120045)
XLA Ops:
  7.4 0.9 slice.7
  8.4 2.4 %collective-permute-start = (bf16[12,16,512]{2,1,0:T(8,128)(2,1)S(1)}, bf16[12,16,512]{2,1,0:T(8,128)(2,1)S(1)}, u32[]{:S(2)}, u32[]{:S(2)}) collective-permute-start(bf16[12,16,512]{2,1,0:T(8,128)(2,1)S(1)} %pad_maximum_fusion), channel_id=1, source_target_pairs={{0,4},{1,5},{2,6},{3,7},{8,12},{9,13},{10,14},{11,15},{16,20},{17,... | collective-permute-start | bytes 589832 | tf_op jit(solution)/shard_map/ppermute | solution.py:21
  10.7 1.0 collective-permute-done.tail_ref
  12.5 4.4 %pack.5 = (bf16[4,272,512]{2,1,0:T(8,128)(2,1)}, bf16[4,256,256]{2,1,0:T(8,128)(2,1)}) custom-call(s32[4,4]{1,0:T(4,128)} %slot_ref.5, s32[1]{0:T(128)S(6)} %min.16.peer_ref, bf16[12,256,256]{2,1,0:T(8,128)(2,1)} %x_ref.5, bf16[12,256,256]{2,1,0:T(8,128)(2,1)} %z_ref.5, bf16[12,256,256]{2,1,0:T(8,128)(2,1)} %bc_ref.5, bf16[12,4,256]{2,1,0:T(4,128)(2,1)} %bitcast.13, ...), custom_call_target="tpu_custom_call" | custom-call | bytes 4000000 | tf_op jit(solution)/shard_map/pack/pallas_call | solution.py:46
  16.9 4.3 %collective-permute-start.1 = (bf16[4,272,512]{2,1,0:T(8,128)(2,1)}, bf16[4,272,512]{2,1,0:T(8,128)(2,1)S(1)}, u32[]{:S(2)}, u32[]{:S(2)}) collective-permute-start(bf16[4,272,512]{2,1,0:T(8,128)(2,1)} %get-tuple-element.22), channel_id=1, source_target_pairs={{0,8},{8,16},{16,24},{1,9},{9,17},{17,25},{2,10},{10,18},{18,26},{... | collective-permute-start | bytes 3342344 | tf_op jit(solution)/shard_map/ppermute | solution.py:21
  21.2 4.5 %pack.4 = (bf16[4,272,512]{2,1,0:T(8,128)(2,1)}, bf16[4,256,256]{2,1,0:T(8,128)(2,1)}) custom-call(s32[4,4]{1,0:T(4,128)} %slot_ref.5, s32[1]{0:T(128)S(6)} %min.15.peer_ref, bf16[12,256,256]{2,1,0:T(8,128)(2,1)} %x_ref.5, bf16[12,256,256]{2,1,0:T(8,128)(2,1)} %z_ref.5, bf16[12,256,256]{2,1,0:T(8,128)(2,1)} %bc_ref.5, bf16[12,4,256]{2,1,0:T(4,128)(2,1)} %bitcast.14, ...), custom_call_target="tpu_custom_call" | custom-call | bytes 4000000 | tf_op jit(solution)/shard_map/pack/pallas_call | solution.py:46
  25.7 1.3 collective-permute-start.2
  27.1 4.5 %pack.3 = (bf16[4,272,512]{2,1,0:T(8,128)(2,1)}, bf16[4,256,256]{2,1,0:T(8,128)(2,1)}) custom-call(s32[4,4]{1,0:T(4,128)} %slot_ref.5, s32[1]{0:T(128)S(6)} %min.14.peer_ref, bf16[12,256,256]{2,1,0:T(8,128)(2,1)} %x_ref.5, bf16[12,256,256]{2,1,0:T(8,128)(2,1)} %z_ref.5, bf16[12,256,256]{2,1,0:T(8,128)(2,1)} %bc_ref.5, bf16[12,4,256]{2,1,0:T(4,128)(2,1)} %bitcast.15, ...), custom_call_target="tpu_custom_call" | custom-call | bytes 4000000 | tf_op jit(solution)/shard_map/pack/pallas_call | solution.py:46
  31.6 14.2 %collective-permute-done.1.left_ref = bf16[4,272,512]{2,1,0:T(8,128)(2,1)S(1)} collective-permute-done((bf16[4,272,512]{2,1,0:T(8,128)(2,1)}, bf16[4,272,512]{2,1,0:T(8,128)(2,1)S(1)}, u32[]{:S(2)}, u32[]{:S(2)}) %collective-permute-start.1) | collective-permute-done | bytes 1114144 | tf_op jit(solution)/shard_map/ppermute | solution.py:21
  45.8 25.7 %collective-permute-done.2.right_ref = bf16[4,272,512]{2,1,0:T(8,128)(2,1)S(1)} collective-permute-done((bf16[4,272,512]{2,1,0:T(8,128)(2,1)}, bf16[4,272,512]{2,1,0:T(8,128)(2,1)S(1)}, u32[]{:S(2)}, u32[]{:S(2)}) %collective-permute-start.2) | collective-permute-done | bytes 1114144 | tf_op jit(solution)/shard_map/ppermute | solution.py:21
  71.5 3.4 %collective-permute-start.4 = (bf16[4,256,256]{2,1,0:T(8,128)(2,1)}, bf16[4,256,256]{2,1,0:T(8,128)(2,1)S(1)}, u32[]{:S(2)}, u32[]{:S(2)}) collective-permute-start(bf16[4,256,256]{2,1,0:T(8,128)(2,1)} %get-tuple-element.31), channel_id=1, source_target_pairs={{0,8},{8,16},{16,24},{1,9},{9,17},{17,25},{2,10},{10,18},{18,26},{... | collective-permute-start | bytes 1572872 | tf_op jit(solution)/shard_map/ppermute | solution.py:21
  74.9 1.3 collective-permute-start.5
  76.3 1.2 copy-done.6
  77.5 6.7 %scan.1 = (f32[4,256,256]{2,1,0:T(8,128)S(1)}, f32[4,256,256]{2,1,0:T(8,128)S(1)}, bf16[4,256,128]{2,1,0:T(8,128)(2,1)S(1)}, f32[4,128,256]{2,1,0:T(8,128)}) custom-call(s32[1]{0:T(128)} %bitcast.rank_ref, s32[4,4]{1,0:T(4,128)S(1)} %copy-done.4, s32[4,4]{1,0:T(4,128)S(1)} %copy-done.5, f32[4]{0:T(128)S(1)} %copy-done.11, f32[4]{0:T(128)S(1)} %copy-done.12, ...), custom_call_target="tpu_custom_call" | custom-call | flops 3000000000 | bytes 8000000 | tf_op jit(solution)/shard_map/scan/pallas_call | solution.py:190
  84.2 1.0 copy-done.1
  85.2 1.0 copy-done.2
  87.0 2.1 %collective-permute-start.3 = (f32[4,128,256]{2,1,0:T(8,128)}, f32[4,128,256]{2,1,0:T(8,128)}, u32[]{:S(2)}, u32[]{:S(2)}) collective-permute-start(f32[4,128,256]{2,1,0:T(8,128)} %get-tuple-element.29), channel_id=1, source_target_pairs={{0,4},{1,5},{2,6},{3,7},{8,12},{9,13},{10,14},{11,15},{16,20},{17,... | collective-permute-start | bytes 1572872 | tf_op jit(solution)/shard_map/ppermute | solution.py:21
  89.0 3.3 %copy.19 = bf16[256,4096]{0,1:T(8,128)(2,1)S(1)} copy(bf16[256,4096]{1,0:T(8,128)(2,1)} %param.31) | data formatting | bytes 4194304 | tf_op args[15]
  92.3 2.4 %copy.20 = bf16[256,4,1024]{2,0,1:T(8,128)(2,1)} copy(bf16[256,4,1024]{0,2,1:T(8,128)(2,1)S(1)} %bitcast.12) | data formatting | bytes 4194304 | tf_op jit(solution)/shard_map/reshape | solution.py:318
  94.7 4.9 %all-to-all-start = ((bf16[4,256,1024]{2,1,0:T(8,128)(2,1)}), bf16[4,256,1024]{2,1,0:T(8,128)(2,1)S(1)}, u32[]{:S(2)}, u32[]{:S(2)}) async-start(bf16[4,256,1024]{2,1,0:T(8,128)(2,1)} %bitcast.11), calls=%async_computation | async-start | bytes 4194304 | tf_op jit(solution)/shard_map/all_to_all | solution.py:319
  100.5 5.5 %gate.1 = bf16[4,256,256]{2,1,0:T(8,128)(2,1)} custom-call(s32[1]{0:T(128)} %bitcast.rank_ref, s32[4,4]{1,0:T(4,128)} %source_ref.3, s32[4,4]{1,0:T(4,128)} %spans_ref.3, f32[4,256,256]{2,1,0:T(8,128)} %copy-done.1, f32[4,256,256]{2,1,0:T(8,128)} %copy-done.2, bf16[4,256,128]{2,1,0:T(8,128)(2,1)} %copy-done.3, ...), custom_call_target="tpu_custom_call" | custom-call | tf_op jit(solution)/shard_map/gate/pallas_call | solution.py:254
  106.1 73.8 %all-to-all-done.weight_ref = bf16[4,256,1024]{2,1,0:T(8,128)(2,1)S(1)} async-done(((bf16[4,256,1024]{2,1,0:T(8,128)(2,1)}), bf16[4,256,1024]{2,1,0:T(8,128)(2,1)S(1)}, u32[]{:S(2)}, u32[]{:S(2)}) %all-to-all-start) | async-done | bytes 2097184 | tf_op jit(solution)/shard_map/all_to_all | solution.py:319
  180.5 1.6 copy-done
  182.1 3.8 %project.1 = bf16[4,256,1024]{2,1,0:T(8,128)(2,1)} custom-call(bf16[4,4,256,256]{3,2,1,0:T(8,128)(2,1)S(1)} %bitcast.8, bf16[4,256,1024]{2,1,0:T(8,128)(2,1)S(1)} %all-to-all-done.weight_ref), custom_call_target="tpu_custom_call" | custom-call | tf_op jit(solution)/shard_map/project/pallas_call | solution.py:279
  (38 shorter events, 4.0 us)
Async XLA Ops:
  8.4 3.4 %collective-permute-start = (bf16[12,16,512]{2,1,0:T(8,128)(2,1)S(1)}, bf16[12,16,512]{2,1,0:T(8,128)(2,1)S(1)}, u32[]{:S(2)}, u32[]{:S(2)}) collective-permute-start(bf16[12,16,512]{2,1,0:T(8,128)(2,1)S(1)} %pad_maximum_fusion), channel_id=1, source_target_pairs={{0,4},{1,5},{2,6},{3,7},{8,12},{9,13},{10,14},{11,15},{16,20},{17,... | collective-permute-start | bytes 589832 | tf_op jit(solution)/shard_map/ppermute | solution.py:21
  16.9 28.9 %collective-permute-start.1 = (bf16[4,272,512]{2,1,0:T(8,128)(2,1)}, bf16[4,272,512]{2,1,0:T(8,128)(2,1)S(1)}, u32[]{:S(2)}, u32[]{:S(2)}) collective-permute-start(bf16[4,272,512]{2,1,0:T(8,128)(2,1)} %get-tuple-element.22), channel_id=1, source_target_pairs={{0,8},{8,16},{16,24},{1,9},{9,17},{17,25},{2,10},{10,18},{18,26},{... | collective-permute-start | bytes 3342344 | tf_op jit(solution)/shard_map/ppermute | solution.py:21
  25.7 45.8 %collective-permute-start.2 = (bf16[4,272,512]{2,1,0:T(8,128)(2,1)}, bf16[4,272,512]{2,1,0:T(8,128)(2,1)S(1)}, u32[]{:S(2)}, u32[]{:S(2)}) collective-permute-start(bf16[4,272,512]{2,1,0:T(8,128)(2,1)} %get-tuple-element.23), channel_id=1, source_target_pairs={{8,0},{16,8},{24,16},{9,1},{17,9},{25,17},{10,2},{18,10},{26,18},{... | collective-permute-start | bytes 3342344 | tf_op jit(solution)/shard_map/ppermute | solution.py:21
  27.0 49.2 %copy-start.4 = (s32[4,4]{1,0:T(4,128)S(1)}, s32[4,4]{1,0:T(4,128)}, u32[]{:S(2)}) copy-start(s32[4,4]{1,0:T(4,128)} %source_ref.3) | copy-start | bytes 196
  27.0 49.2 %copy-start.5 = (s32[4,4]{1,0:T(4,128)S(1)}, s32[4,4]{1,0:T(4,128)}, u32[]{:S(2)}) copy-start(s32[4,4]{1,0:T(4,128)} %spans_ref.3) | copy-start | bytes 196
  27.0 49.2 %copy-start.7 = (f32[4,256]{1,0:T(4,128)S(1)}, f32[4,256]{1,0:T(4,128)}, u32[]{:S(2)}) copy-start(f32[4,256]{1,0:T(4,128)} %wx_ref.1) | copy-start | bytes 12292
  27.0 49.2 %copy-start.8 = (f32[4,256]{1,0:T(4,128)S(1)}, f32[4,256]{1,0:T(4,128)}, u32[]{:S(2)}) copy-start(f32[4,256]{1,0:T(4,128)} %wbc_ref.1) | copy-start | bytes 12292
  27.0 49.2 %copy-start.9 = (f32[256]{0:T(256)S(1)}, f32[256]{0:T(256)}, u32[]{:S(2)}) copy-start(f32[256]{0:T(256)} %param.24) | copy-start | bytes 3076
  27.0 49.2 %copy-start.10 = (f32[256]{0:T(256)S(1)}, f32[256]{0:T(256)}, u32[]{:S(2)}) copy-start(f32[256]{0:T(256)} %param.26) | copy-start | bytes 3076
  27.0 49.2 %copy-start.11 = (f32[4]{0:T(128)S(1)}, f32[4]{0:T(128)}, u32[]{:S(2)}) copy-start(f32[4]{0:T(128)} %dtb_ref.1) | copy-start | bytes 52
  27.0 49.2 %copy-start.12 = (f32[4]{0:T(128)S(1)}, f32[4]{0:T(128)}, u32[]{:S(2)}) copy-start(f32[4]{0:T(128)} %alog_ref.1) | copy-start | bytes 52
  27.1 49.2 %copy-start.13 = (f32[4]{0:T(128)S(1)}, f32[4]{0:T(128)}, u32[]{:S(2)}) copy-start(f32[4]{0:T(128)} %skip_ref.1) | copy-start | bytes 52
  71.5 28.1 %collective-permute-start.4 = (bf16[4,256,256]{2,1,0:T(8,128)(2,1)}, bf16[4,256,256]{2,1,0:T(8,128)(2,1)S(1)}, u32[]{:S(2)}, u32[]{:S(2)}) collective-permute-start(bf16[4,256,256]{2,1,0:T(8,128)(2,1)} %get-tuple-element.31), channel_id=1, source_target_pairs={{0,8},{8,16},{16,24},{1,9},{9,17},{17,25},{2,10},{10,18},{18,26},{... | collective-permute-start | bytes 1572872 | tf_op jit(solution)/shard_map/ppermute | solution.py:21
  74.9 24.7 %collective-permute-start.5 = (bf16[4,256,256]{2,1,0:T(8,128)(2,1)}, bf16[4,256,256]{2,1,0:T(8,128)(2,1)S(1)}, u32[]{:S(2)}, u32[]{:S(2)}) collective-permute-start(bf16[4,256,256]{2,1,0:T(8,128)(2,1)} %get-tuple-element.32), channel_id=1, source_target_pairs={{8,0},{16,8},{24,16},{9,1},{17,9},{25,17},{10,2},{18,10},{26,18},{... | collective-permute-start | bytes 1572872 | tf_op jit(solution)/shard_map/ppermute | solution.py:21
  76.3 1.3 copy-start.6
  84.2 1.0 copy-start.1
  85.2 1.0 copy-start.2
  86.2 0.7 copy-start.3
  87.0 12.6 %collective-permute-start.3 = (f32[4,128,256]{2,1,0:T(8,128)}, f32[4,128,256]{2,1,0:T(8,128)}, u32[]{:S(2)}, u32[]{:S(2)}) collective-permute-start(f32[4,128,256]{2,1,0:T(8,128)} %get-tuple-element.29), channel_id=1, source_target_pairs={{0,4},{1,5},{2,6},{3,7},{8,12},{9,13},{10,14},{11,15},{16,20},{17,... | collective-permute-start | bytes 1572872 | tf_op jit(solution)/shard_map/ppermute | solution.py:21
  94.7 85.2 %all-to-all-start = ((bf16[4,256,1024]{2,1,0:T(8,128)(2,1)}), bf16[4,256,1024]{2,1,0:T(8,128)(2,1)S(1)}, u32[]{:S(2)}, u32[]{:S(2)}) async-start(bf16[4,256,1024]{2,1,0:T(8,128)(2,1)} %bitcast.11), calls=%async_computation | async-start | bytes 4194304 | tf_op jit(solution)/shard_map/all_to_all | solution.py:319
  99.6 80.9 %all-gather.3.cloned.1.call-start = ((), (), s32[]{:S(2)}) async-start(), calls=%async_computation.1 | async-start | bytes 2621440 | tf_op jit(solution)/shard_map/all_gather | solution.py:334
  99.6 0.8 copy-start.15
  99.6 1.0 copy-start.16
  180.5 1.6 copy-start
  (1 other events, 0.7 us)
Sparse Core Ops, SparseCore 0:
  106.2 74.2 all-gather.2
where the time goes:
time: 194 us; the launch traced here: 193 us
  waiting for transfers between devices  115 us (59%)
  Pallas kernels  29.5 us (15%)
  starting transfers between devices  19.6 us (10%)
  local copies, waits for them, and re-layouts  14.7 us (8%)
  between operations  13.7 us (7%)
    all_to_all x1, waiting for transfers between devices, body(): weight = lax.all_to_all(pieces, 'tensor', 0, 0, tiled=True)  73.8 us
    ppermute x6, waiting for transfers between devices, shifted(): lax.ppermute(value, axis, [(source, source + steps) for source in range(f...  40.9 us
    ppermute x6, starting transfers between devices, shifted(): lax.ppermute(value, axis, [(source, source + steps) for source in range(f...  14.7 us
    pallas_call x3, Pallas kernels, pack(): pl.pallas_call(pack_kernel, grid_spec=pltpu.PrefetchScalarGridSpec(num_sc...  13.4 us
    unnamed x35, local copies, waits for them, and re-layouts  10.5 us
    pallas_call x1, Pallas kernels, scan(): pl.pallas_call(scan_kernel, grid_spec=pltpu.PrefetchScalarGridSpec(num_sc...  6.67 us
    pallas_call x1, Pallas kernels, gate(): pl.pallas_call(gate_kernel, grid_spec=pltpu.PrefetchScalarGridSpec(num_sc...  5.5 us
    all_to_all x1, starting transfers between devices, body(): weight = lax.all_to_all(pieces, 'tensor', 0, 0, tiled=True)  4.87 us
  transfers between devices with their start and end apart: 8, of which 5 were waited for; matrix products, arithmetic and copies ran while one was open for 3% of the time, Pallas kernels for 11%

commit v1 on v0

--- a/solution.py
+++ b/solution.py
@@ -1,5 +1,3 @@
-import functools
-
 import jax
 import jax.numpy as jnp
 from jax import lax
@@ -12,7 +10,6 @@
 EPS = 1e-05
 F32 = jnp.float32
 BF16 = jnp.bfloat16
-HIGHEST = lax.Precision.HIGHEST
 
 
 def shifted(value, axis, steps):
@@ -21,43 +18,166 @@
     return lax.ppermute(value, axis, [(source, source + steps) for source in range(first, last)])
 
 
-def pack_kernel(slot_ref, peer_ref, x_ref, z_ref, bc_ref, dt_ref, tail_ref, main_ref, gate_ref):
+MESH = pl.DeviceIdType.MESH
+ANY = pl.BlockSpec(memory_space=pl.ANY)
+VMEM = pl.BlockSpec(memory_space=pltpu.VMEM)
+SMEM = pl.BlockSpec(memory_space=pltpu.SMEM)
+
+
+def exchange_kernel(
+    slot_ref, x_ref, z_ref, bc_ref, dt_ref, weight_in,
+    own_ref, left_ref, right_ref, own_gate, up_gate, down_gate, weight_ref,
+    tail_x, tail_bc, send, tail_send, tail_recv, move_send, move_recv, part_send, part_recv, local,
+):
+    ranks, pieces, groups = (lax.axis_size(axis) for axis in ("dp", "seq", "tensor"))
+    d, q, m = (lax.axis_index(axis) for axis in ("dp", "seq", "tensor"))
+    count = slot_ref.shape[1]
     length, width = x_ref.shape[1:]
     heads = dt_ref.shape[1]
-    main_ref[0, :length, :width] = x_ref[0]
-    main_ref[0, :length, width:] = bc_ref[0]
-    main_ref[0, length:, :] = tail_ref[0]
-    main_ref[0, length : length + heads, : dt_ref.shape[2]] = dt_ref[0]
-    gate_ref[0] = z_ref[0]
-
-
-def pack(source_slot, peer, entry_x, entry_z, entry_bc, dt_rows, tails):
+    cols = weight_ref.shape[2]
+
+    barrier = pltpu.get_barrier_semaphore()
+    near = (
+        (d > 0, {"dp": d - 1}), (d < ranks - 1, {"dp": d + 1}),
+        (q > 0, {"seq": q - 1}), (q < pieces - 1, {"seq": q + 1}),
+    )
+    for there, target in near:
+        @pl.when(there)
+        def _(target=target):
+            pl.semaphore_signal(barrier, inc=1, device_id=target, device_id_type=MESH)
+    for k in range(1, groups):
+        peer = lax.rem(m + k, groups)
+        pl.semaphore_signal(barrier, inc=1, device_id={"tensor": peer}, device_id_type=MESH)
+    pl.semaphore_wait(barrier, groups - 1 + sum(there.astype(jnp.int32) for there, _ in near))
+
+    def tail_copies():
+        ends = pl.ds(length - EXTRA, EXTRA)
+        target = {"seq": q + 1}
+        return [
+            pltpu.make_async_remote_copy(
+                ref.at[:, ends, :], dst, tail_send.at[i], tail_recv.at[i],
+                device_id=target, device_id_type=MESH,
+            )
+            for i, (ref, dst) in enumerate(((x_ref, tail_x), (bc_ref, tail_bc)))
+        ]
+
+    def move(side, j):
+        dst = (right_ref, left_ref)[side]
+        return pltpu.make_async_remote_copy(
+            send.at[side, j], dst.at[j], move_send.at[side, j], move_recv.at[side, j],
+            device_id={"dp": d + (2 * side - 1)}, device_id_type=MESH,
+        )
+
+    def part(k):
+        peer = lax.rem(m + k, groups)
+        return pltpu.make_async_remote_copy(
+            weight_in.at[:, pl.ds(pl.multiple_of(peer * cols, cols), cols)],
+            weight_ref.at[m], part_send.at[k - 1], part_recv.at[k - 1],
+            device_id={"tensor": peer}, device_id_type=MESH,
+        )
+
+    def arrived(k):
+        peer = lax.rem(m - k + groups, groups)
+        return pltpu.make_async_remote_copy(
+            weight_in.at[:, pl.ds(0, cols)],
+            weight_ref.at[peer], part_send.at[k - 1], part_recv.at[k - 1],
+            device_id={"tensor": peer}, device_id_type=MESH,
+        )
+
+    @pl.when(q < pieces - 1)
+    def _():
+        for copy in tail_copies():
+            copy.start()
+
+    keep = pltpu.make_async_copy(
+        weight_in.at[:, pl.ds(pl.multiple_of(m * cols, cols), cols)], weight_ref.at[m], local.at[0]
+    )
+    keep.start()
+    for k in range(1, groups):
+        part(k).start()
+
+    @pl.when(q == 0)
+    def _():
+        tail_x[...] = jnp.zeros_like(tail_x)
+        tail_bc[...] = jnp.zeros_like(tail_bc)
+
+    @pl.when(q > 0)
+    def _():
+        for copy in tail_copies():
+            copy.wait_recv()
+
+    def fill(ref, at, slot):
+        ref[at + (slice(0, length), slice(0, width))] = x_ref[slot]
+        ref[at + (slice(0, length), slice(width, None))] = bc_ref[slot]
+        ref[at + (slice(length, None), slice(0, width))] = tail_x[slot]
+        ref[at + (slice(length, None), slice(width, None))] = tail_bc[slot]
+        ref[at + (slice(length, length + heads), slice(0, length))] = dt_ref[slot]
+
+    sides = ((d > 0, jnp.maximum(d - 1, 0)), (d < ranks - 1, jnp.minimum(d + 1, ranks - 1)))
+    for j in range(count):
+        for side, (there, peer) in enumerate(sides):
+            fill(send, (side, j), slot_ref[peer, j])
+
+            @pl.when(there)
+            def _(side=side, j=j):
+                move(side, j).start()
+    for j in range(count):
+        fill(own_ref, (j,), slot_ref[d, j])
+        own_gate[j] = z_ref[slot_ref[d, j]]
+        down_gate[j] = z_ref[slot_ref[sides[0][1], j]]
+        up_gate[j] = z_ref[slot_ref[sides[1][1], j]]
+
+    for side in range(2):
+        there, back = sides[side][0], sides[1 - side][0]
+        for j in range(count):
+            @pl.when(there)
+            def _(side=side, j=j):
+                move(side, j).wait_send()
+
+            @pl.when(back)
+            def _(side=side, j=j):
+                move(side, j).wait_recv()
+
+    @pl.when(q < pieces - 1)
+    def _():
+        for copy in tail_copies():
+            copy.wait_send()
+
+    keep.wait()
+    for k in range(1, groups):
+        part(k).wait_send()
+        arrived(k).wait_recv()
+
+
+def exchange(source_slot, entry_x, entry_z, entry_bc, dt_rows, out_weight, groups):
     count = source_slot.shape[1]
-    length, width = entry_x.shape[1:]
-    full = width + entry_bc.shape[2]
-
-    def spec(array):
-        return pl.BlockSpec((1,) + array.shape[1:], lambda j, slots, who: (slots[who[0], j], 0, 0))
-
-    def out(rows, cols):
-        return pl.BlockSpec((1, rows, cols), lambda j, slots, who: (j, 0, 0))
-
-    operands = (entry_x, entry_z, entry_bc, dt_rows, tails)
+    slots, length, width = entry_x.shape
+    bc_width = entry_bc.shape[2]
+    full = width + bc_width
+    cols = out_weight.shape[1] // groups
+    main = jax.ShapeDtypeStruct((count, length + EXTRA, full), BF16)
+    small = jax.ShapeDtypeStruct((count, length, width), BF16)
+    dma = pltpu.SemaphoreType.DMA
     return pl.pallas_call(
-        pack_kernel,
-        grid_spec=pltpu.PrefetchScalarGridSpec(
-            num_scalar_prefetch=2,
-            grid=(count,),
-            in_specs=[spec(array) for array in operands],
-            out_specs=[out(length + EXTRA, full), out(length, width)],
+        exchange_kernel,
+        in_specs=[SMEM, VMEM, VMEM, VMEM, VMEM, ANY],
+        out_specs=[VMEM, ANY, ANY, VMEM, VMEM, VMEM, ANY],
+        out_shape=[
+            main, main, main, small, small, small,
+            jax.ShapeDtypeStruct((groups, width, cols), BF16),
+        ],
+        scratch_shapes=[
+            pltpu.VMEM((slots, EXTRA, width), BF16),
+            pltpu.VMEM((slots, EXTRA, bc_width), BF16),
+            pltpu.VMEM((2, count, length + EXTRA, full), BF16),
+            dma((2,)), dma((2,)), dma((2, count)), dma((2, count)),
+            dma((max(groups - 1, 1),)), dma((max(groups - 1, 1),)), dma((1,)),
+        ],
+        compiler_params=pltpu.CompilerParams(
+            collective_id=0, has_side_effects=True, vmem_limit_bytes=40 << 20
         ),
-        out_shape=[
-            jax.ShapeDtypeStruct((count, length + EXTRA, full), BF16),
-            jax.ShapeDtypeStruct((count, length, width), BF16),
-        ],
-        cost_estimate=pl.CostEstimate(flops=0, bytes_accessed=4_000_000, transcendentals=0),
-        name="pack",
-    )(source_slot, peer, *operands)
+        name="exchange",
+    )(source_slot, entry_x, entry_z, entry_bc, dt_rows, out_weight)
 
 
 def slot_row(spans_ref, rank, j, count):
@@ -220,74 +340,109 @@
     )(rank, source_rank, row_spans, dt_bias, a_log, d_skip, own, left, right, wx, wbc, bx, bbc)
 
 
-def gate_kernel(
+def finish_kernel(
     rank_ref, source_ref, spans_ref,
-    base_ref, scale_ref, c_ref, carried_ref, own_ref, left_ref, right_ref, gain_ref, out_ref,
+    base_ref, scale_ref, c_ref, carried_ref, own_ref, left_ref, right_ref, gain_ref, weight_ref,
+    out_ref, rows, right_send, left_send, arrive,
 ):
-    j = pl.program_id(0)
+    groups = weight_ref.shape[0]
+    count = base_ref.shape[0]
     rank = rank_ref[0]
-    _, final = slot_row(spans_ref, rank, j, carried_ref.shape[0])
-    carried = carried_ref[final]
-    high = carried.astype(BF16)
-    low = (carried - high.astype(F32)).astype(BF16)
-    c_act = c_ref[0]
-    read = jnp.dot(c_act, high, preferred_element_type=F32) + jnp.dot(
-        c_act, low, preferred_element_type=F32
-    )
-    y = base_ref[0] + scale_ref[0] * read
-    parts = [ref[0].astype(F32) for ref in (own_ref, left_ref, right_ref)]
-    z = choose(source_ref[rank, j], rank, *parts)
-    g = y * (z / (1.0 + jnp.exp(-z)))
-    inverse = lax.rsqrt(jnp.mean(g * g, axis=-1, keepdims=True) + EPS)
-    out_ref[0] = (g * inverse * gain_ref[...]).astype(BF16)
-
-
-def gate(rank, source_rank, row_spans, base, scale, c_act, carried, own, left, right, gain):
+    m = lax.axis_index("tensor")
+    barrier = pltpu.get_barrier_semaphore()
+    near = ((m > 0, m - 1), (m < groups - 1, m + 1))
+    for there, peer in near:
+        @pl.when(there)
+        def _(peer=peer):
+            pl.semaphore_signal(barrier, inc=1, device_id={"tensor": peer}, device_id_type=MESH)
+    pl.semaphore_wait(barrier, sum(there.astype(jnp.int32) for there, _ in near))
+
+    def hop(side, source, j):
+        return pltpu.make_async_remote_copy(
+            rows.at[source, j], rows.at[source, j],
+            (left_send, right_send)[side].at[source, j], arrive.at[source, j],
+            device_id={"tensor": m + (2 * side - 1)}, device_id_type=MESH,
+        )
+
+    for j in range(count):
+        _, final = slot_row(spans_ref, rank, jnp.int32(j), count)
+        carried = carried_ref[final]
+        high = carried.astype(BF16)
+        low = (carried - high.astype(F32)).astype(BF16)
+        c_act = c_ref[j]
+        read = jnp.dot(c_act, high, preferred_element_type=F32) + jnp.dot(
+            c_act, low, preferred_element_type=F32
+        )
+        y = base_ref[j] + scale_ref[j] * read
+        parts = [ref[j].astype(F32) for ref in (own_ref, left_ref, right_ref)]
+        z = choose(source_ref[rank, j], rank, *parts)
+        g = y * (z / (1.0 + jnp.exp(-z)))
+        inverse = lax.rsqrt(jnp.mean(g * g, axis=-1, keepdims=True) + EPS)
+        rows[m, j] = (g * inverse * gain_ref[...]).astype(BF16)
+        for side, (there, _) in enumerate(near):
+            @pl.when(there)
+            def _(side=side, j=j):
+                hop(side, m, j).start()
+
+    def one_slot(j, token):
+        for k in range(1, groups):
+            for side in range(2):
+                source = m - k if side == 1 else m + k
+                here = (source >= 0) if side == 1 else (source < groups)
+
+                @pl.when(here)
+                def _(side=side, source=source):
+                    hop(side, source, j).wait_recv()
+
+                @pl.when(here & near[side][0])
+                def _(side=side, source=source):
+                    hop(side, source, j).start()
+        total = jnp.dot(rows[0, j], weight_ref[0], preferred_element_type=F32)
+        for i in range(1, groups):
+            total = total + jnp.dot(rows[i, j], weight_ref[i], preferred_element_type=F32)
+        out_ref[j] = total.astype(BF16)
+        return token
+
+    lax.fori_loop(0, count, one_slot, 0)
+
+    def drain(j, token):
+        for side, (there, _) in enumerate(near):
+            @pl.when(there)
+            def _(side=side):
+                hop(side, m, j).wait_send()
+        for k in range(1, groups):
+            for side in range(2):
+                source = m - k if side == 1 else m + k
+                here = (source >= 0) if side == 1 else (source < groups)
+
+                @pl.when(here & near[side][0])
+                def _(side=side, source=source):
+                    hop(side, source, j).wait_send()
+        return token
+
+    lax.fori_loop(0, count, drain, 0)
+
+
+def finish(
+    rank, source_rank, row_spans, base, scale, c_act, carried, own, left, right, gain, weight
+):
     count, length, width = base.shape
-
-    def whole(array):
-        return pl.BlockSpec(array.shape, lambda j, *_: (0,) * array.ndim)
-
-    def slot(array):
-        return pl.BlockSpec((1,) + array.shape[1:], lambda j, *_: (j, 0, 0))
-
+    groups, _, cols = weight.shape
+    dma = pltpu.SemaphoreType.DMA
     return pl.pallas_call(
-        gate_kernel,
-        grid_spec=pltpu.PrefetchScalarGridSpec(
-            num_scalar_prefetch=3,
-            grid=(count,),
-            in_specs=[slot(base), slot(scale), slot(c_act), whole(carried)]
-            + [slot(own)] * 3
-            + [whole(gain)],
-            out_specs=slot(base),
+        finish_kernel,
+        in_specs=[SMEM] * 3 + [VMEM] * 9,
+        out_specs=VMEM,
+        out_shape=jax.ShapeDtypeStruct((count, length, cols), BF16),
+        scratch_shapes=[
+            pltpu.VMEM((groups, count, length, width), BF16),
+            dma((groups, count)), dma((groups, count)), dma((groups, count)),
+        ],
+        compiler_params=pltpu.CompilerParams(
+            collective_id=1, has_side_effects=True, vmem_limit_bytes=48 << 20
         ),
-        out_shape=jax.ShapeDtypeStruct((count, length, width), BF16),
-        name="gate",
-    )(rank, source_rank, row_spans, base, scale, c_act, carried, own, left, right, gain)
-
-
-def project_kernel(rows_ref, weight_ref, out_ref):
-    total = jnp.dot(rows_ref[0, 0], weight_ref[0], preferred_element_type=F32)
-    for i in range(1, weight_ref.shape[0]):
-        total = total + jnp.dot(rows_ref[i, 0], weight_ref[i], preferred_element_type=F32)
-    out_ref[0] = total.astype(BF16)
-
-
-def project(rows, weight):
-    groups, count, length, width = rows.shape
-    cols = weight.shape[2]
-    return pl.pallas_call(
-        project_kernel,
-        grid=(count,),
-        in_specs=[
-            pl.BlockSpec((groups, 1, length, width), lambda j: (0, j, 0, 0)),
-            pl.BlockSpec(weight.shape, lambda j: (0, 0, 0)),
-        ],
-        out_specs=pl.BlockSpec((1, length, cols), lambda j: (j, 0, 0)),
-        out_shape=jax.ShapeDtypeStruct((count, length, cols), BF16),
-        compiler_params=pltpu.CompilerParams(vmem_limit_bytes=40 << 20),
-        name="project",
-    )(rows, weight)
+        name="finish",
+    )(rank, source_rank, row_spans, base, scale, c_act, carried, own, left, right, gain, weight)
 
 
 def body(
@@ -295,30 +450,14 @@
     conv_x_weight, conv_x_bias, conv_bc_weight, conv_bc_bias,
     dt_bias, a_log, d_skip, norm_gain, out_weight,
 ):
-    length, width = entry_x.shape[1:]
-    ranks, groups = lax.axis_size("dp"), lax.axis_size("tensor")
+    groups = lax.axis_size("tensor")
     me = lax.axis_index("dp").astype(jnp.int32)
     rank = me.reshape(1)
 
     dt_rows = jnp.swapaxes(entry_dt, 1, 2)
-    ends = jnp.concatenate([entry_x[:, length - EXTRA :], entry_bc[:, length - EXTRA :]], 2)
-    tails = shifted(ends, "seq", 1)
-
-    def packed(peer):
-        peer = jnp.clip(peer, 0, ranks - 1).astype(jnp.int32)
-        return pack(source_slot, peer, entry_x, entry_z, entry_bc, dt_rows, tails)
-
-    down_main, down_gate = packed(rank - 1)
-    up_main, up_gate = packed(rank + 1)
-    right = shifted(down_main, "dp", -1)
-    left = shifted(up_main, "dp", 1)
-    own, own_gate = packed(rank)
-
-    cols = out_weight.shape[1] // groups
-    pieces = jnp.swapaxes(out_weight.reshape(width, groups, cols), 0, 1)
-    weight = lax.all_to_all(pieces, "tensor", 0, 0, tiled=True)
-
-    down_gate, up_gate, left, right = lax.optimization_barrier((down_gate, up_gate, left, right))
+    own, left, right, own_gate, up_gate, down_gate, weight = exchange(
+        source_slot, entry_x, entry_z, entry_bc, dt_rows, out_weight, groups
+    )
     right_gate = shifted(down_gate, "dp", -1)
     left_gate = shifted(up_gate, "dp", 1)
 
@@ -327,12 +466,10 @@
         conv_x_weight, conv_bc_weight, conv_x_bias.reshape(1, -1), conv_bc_bias.reshape(1, -1),
     )
     carried = shifted(ended, "seq", 1)
-    normed = gate(
+    return finish(
         rank, source_rank, row_spans, base, scale, c_act, carried,
-        own_gate, left_gate, right_gate, norm_gain.reshape(1, -1),
-    )
-    gathered = lax.all_gather(normed, "tensor", axis=0)
-    return project(gathered, weight)
+        own_gate, left_gate, right_gate, norm_gain.reshape(1, -1), weight,
+    )
 
 
 def solution(mesh):

time: 194 us -> 143 us (0.74)
  waiting for transfers between devices: 115 us -> 24.1 us
  Pallas kernels: 29.5 us -> 96.2 us
  between operations: 13.7 us -> 0.2 us
  starting transfers between devices: 19.6 us -> 11.4 us
  local copies, waits for them, and re-layouts: 14.7 us -> 10.4 us
    all_to_all x1 -> x0, waiting for transfers between devices: 73.8 us -> none  [body(): weight = lax.all_to_all(pieces, 'tensor', 0, 0, tiled=True)]
    pallas_call x5 -> x2, Pallas kernels: 22.8 us -> 90.1 us  [the longest x1 50.3 us: exchange(): pl.pallas_call(exchange_kernel, in_specs=[SMEM, VMEM, VMEM, VMEM, VMEM, A...]
    ppermute x6 -> x3, waiting for transfers between devices: 40.9 us -> 24.1 us  [shifted(): lax.ppermute(value, axis, [(source, source + steps) for source in range(f...]
    all_to_all x1 -> x0, starting transfers between devices: 4.87 us -> none  [body(): weight = lax.all_to_all(pieces, 'tensor', 0, 0, tiled=True)]
    ppermute x6 -> x3, starting transfers between devices: 14.7 us -> 11.4 us  [shifted(): lax.ppermute(value, axis, [(source, source + steps) for source in range(f...]
    reshape x1 -> x0, local copies, waits for them, and re-layouts: 2.38 us -> none  [body(): pieces = jnp.swapaxes(out_weight.reshape(width, groups, cols), 0, 1)]
  transfers between devices with their start and end apart: 8 -> 3, of which waited for: 5 -> 2; matrix products, arithmetic and copies ran while one was open for 3% -> 0% of each run, Pallas kernels for 11% -> 0%
where the time goes in v1:
time: 143 us; the launch traced here: 142 us
  Pallas kernels  96.2 us (67%)
  waiting for transfers between devices  24.1 us (17%)
  starting transfers between devices  11.4 us (8%)
  local copies, waits for them, and re-layouts  10.4 us (7%)
    pallas_call x1, Pallas kernels, exchange(): pl.pallas_call(exchange_kernel, in_specs=[SMEM, VMEM, VMEM, VMEM, VMEM, A...  50.3 us
    pallas_call x1, Pallas kernels, finish(): pl.pallas_call(finish_kernel, in_specs=[SMEM] * 3 + [VMEM] * 9, out_specs...  39.9 us
    ppermute x3, waiting for transfers between devices, shifted(): lax.ppermute(value, axis, [(source, source + steps) for source in range(f...  24.1 us
    ppermute x3, starting transfers between devices, shifted(): lax.ppermute(value, axis, [(source, source + steps) for source in range(f...  11.4 us
    unnamed x35, local copies, waits for them, and re-layouts  10.4 us
    pallas_call x1, Pallas kernels, scan(): pl.pallas_call(scan_kernel, grid_spec=pltpu.PrefetchScalarGridSpec(num_sc...  6.12 us
  transfers between devices with their start and end apart: 3, of which 2 were waited for; matrix products, arithmetic and copies ran while one was open for 0% of the time, Pallas kernels for 0%

profile of v1, /device:TPU:0, one launch (start us, length us, event | category | flops | bytes accessed | tf_op | source)
XLA Modules:
  0.0 142.3 jit_solution(53927519710526706)
XLA Ops:
  0.0 1.6 %copy-done = bf16[256,4096]{1,0:T(8,128)(2,1)S(1)} copy-done((bf16[256,4096]{1,0:T(8,128)(2,1)S(1)}, bf16[256,4096]{1,0:T(8,128)(2,1)}, u32[]{:S(2)}) %copy-start) | copy-done | bytes 2097176
  1.6 1.4 copy-done.2
  3.0 1.4 copy-done.3
  4.4 1.4 copy-done.4
  5.8 0.7 copy-done.5
  6.6 0.7 copy-done.6
  7.2 0.0 copy-start.12
  7.3 0.0 copy-start.13
  7.3 0.0 copy-start.14
  7.3 0.0 copy-start.15
  7.3 0.0 copy-start.16
  7.3 50.3 %exchange.1 = (bf16[4,272,512]{2,1,0:T(8,128)(2,1)S(1)}, bf16[4,272,512]{2,1,0:T(8,128)(2,1)S(1)}, bf16[4,272,512]{2,1,0:T(8,128)(2,1)S(1)}, bf16[4,256,256]{2,1...) custom-call(s32[4,4]{1,0:T(4,128)S(1)} %copy-done.6, ...), custom_call_target="tpu_custom_call" | custom-call | tf_op jit(solution)/shard_map/exchange/pallas_call | solution.py:161
  57.6 0.0 copy-start.1
  57.6 0.0 copy-done.7
  57.7 0.0 copy-start.9
  57.7 6.1 %scan.1 = (f32[4,256,256]{2,1,0:T(8,128)S(1)}, f32[4,256,256]{2,1,0:T(8,128)S(1)}, bf16[4,256,128]{2,1,0:T(8,128)(2,1)S(1)}, f32[4,128,256]{2,1,0:T(8,128)S(1)}) custom-call(s32[1]{0:T(128)} %bitcast.rank_ref, s32[4,4]{1,0:T(4,128)S(1)} %copy-done.7, s32[4,4]{1,0:T(4,128)S(1)} %copy-done.8, f32[4]{0:T(128)S(1)} %copy-done.14, f32[4]{0:T(128)S(1)} %copy-done.15, ...), custom_call_target="tpu_custom_call" | custom-call | flops 3000000000 | bytes 8000000 | tf_op jit(solution)/shard_map/scan/pallas_call | solution.py:310
  63.8 3.0 %collective-permute-start = (f32[4,128,256]{2,1,0:T(8,128)S(1)}, f32[4,128,256]{2,1,0:T(8,128)S(1)}, u32[]{:S(2)}, u32[]{:S(2)}) collective-permute-start(f32[4,128,256]{2,1,0:T(8,128)S(1)} %get-tuple-element.22), channel_id=1, source_target_pairs={{0,4},{1,5},{2,6},{3,7},{8,12},{9,13},{10,14},{11,15},{16,20},{17,... | collective-permute-start | bytes 1572872 | tf_op jit(solution)/shard_map/ppermute | solution.py:18
  66.8 7.1 %collective-permute-start.1 = (bf16[4,256,256]{2,1,0:T(8,128)(2,1)S(1)}, bf16[4,256,256]{2,1,0:T(8,128)(2,1)S(1)}, u32[]{:S(2)}, u32[]{:S(2)}) collective-permute-start(bf16[4,256,256]{2,1,0:T(8,128)(2,1)S(1)} %get-tuple-element.24), channel_id=1, source_target_pairs={{0,8},{8,16},{16,24},{1,9},{9,17},{17,25},{2,10},{10,18},{18,26},{... | collective-permute-start | bytes 1572872 | tf_op jit(solution)/shard_map/ppermute | solution.py:18
  73.9 1.3 collective-permute-start.2
  75.2 0.0 collective-permute-done.carried_ref
  75.3 9.3 %collective-permute-done.1.left_ref = bf16[4,256,256]{2,1,0:T(8,128)(2,1)S(1)} collective-permute-done((bf16[4,256,256]{2,1,0:T(8,128)(2,1)S(1)}, bf16[4,256,256]{2,1,0:T(8,128)(2,1)S(1)}, u32[]{:S(2)}, u32[]{:S(2)}) %collective-permute-start.1) | collective-permute-done | bytes 524320 | tf_op jit(solution)/shard_map/ppermute | solution.py:18
  84.6 14.8 %collective-permute-done.2.right_ref = bf16[4,256,256]{2,1,0:T(8,128)(2,1)S(1)} collective-permute-done((bf16[4,256,256]{2,1,0:T(8,128)(2,1)S(1)}, bf16[4,256,256]{2,1,0:T(8,128)(2,1)S(1)}, u32[]{:S(2)}, u32[]{:S(2)}) %collective-permute-start.2) | collective-permute-done | bytes 524320 | tf_op jit(solution)/shard_map/ppermute | solution.py:18
  99.4 39.9 %finish.1 = bf16[4,256,1024]{2,1,0:T(8,128)(2,1)} custom-call(s32[1]{0:T(128)} %bitcast.rank_ref, s32[4,4]{1,0:T(4,128)S(1)} %copy-done.7, s32[4,4]{1,0:T(4,128)S(1)} %copy-done.8, f32[4,256,256]{2,1,0:T(8,128)S(1)} %get-tuple-element.19.base_ref, f32[4,256,256]{2,1,0:T(8,128)S(1)} %get-tuple-element.20.scale_ref, ...), custom_call_target="tpu_custom_call" | custom-call | tf_op jit(solution)/shard_map/finish/pallas_call | solution.py:432
  139.2 3.1 %copy.18 = bf16[4,256,1024]{2,1,0:T(8,128)(2,1)} copy(bf16[4,256,1024]{2,1,0:T(8,128)(2,1)} %finish.1) | data formatting | bytes 4194304
  (20 shorter events, 0.0 us)
Async XLA Ops:
  0.0 1.6 %copy-start = (bf16[256,4096]{1,0:T(8,128)(2,1)S(1)}, bf16[256,4096]{1,0:T(8,128)(2,1)}, u32[]{:S(2)}) copy-start(bf16[256,4096]{1,0:T(8,128)(2,1)} %weight_in.1) | copy-start | bytes 6291460
  1.6 1.4 copy-start.2
  3.0 1.4 copy-start.3
  4.4 1.4 copy-start.4
  5.8 0.7 copy-start.5
  6.6 0.7 copy-start.6
  7.2 50.3 %copy-start.7 = (s32[4,4]{1,0:T(4,128)S(1)}, s32[4,4]{1,0:T(4,128)}, u32[]{:S(2)}) copy-start(s32[4,4]{1,0:T(4,128)} %source_ref.3) | copy-start | bytes 196
  7.2 50.3 %copy-start.8 = (s32[4,4]{1,0:T(4,128)S(1)}, s32[4,4]{1,0:T(4,128)}, u32[]{:S(2)}) copy-start(s32[4,4]{1,0:T(4,128)} %spans_ref.3) | copy-start | bytes 196
  7.2 50.4 %copy-start.10 = (f32[4,256]{1,0:T(4,128)S(1)}, f32[4,256]{1,0:T(4,128)}, u32[]{:S(2)}) copy-start(f32[4,256]{1,0:T(4,128)} %wx_ref.1) | copy-start | bytes 12292
  7.2 50.4 %copy-start.11 = (f32[4,256]{1,0:T(4,128)S(1)}, f32[4,256]{1,0:T(4,128)}, u32[]{:S(2)}) copy-start(f32[4,256]{1,0:T(4,128)} %wbc_ref.1) | copy-start | bytes 12292
  7.2 50.4 %copy-start.12 = (f32[256]{0:T(256)S(1)}, f32[256]{0:T(256)}, u32[]{:S(2)}) copy-start(f32[256]{0:T(256)} %param.24) | copy-start | bytes 3076
  7.3 50.4 %copy-start.13 = (f32[256]{0:T(256)S(1)}, f32[256]{0:T(256)}, u32[]{:S(2)}) copy-start(f32[256]{0:T(256)} %param.26) | copy-start | bytes 3076
  7.3 50.4 %copy-start.14 = (f32[4]{0:T(128)S(1)}, f32[4]{0:T(128)}, u32[]{:S(2)}) copy-start(f32[4]{0:T(128)} %dtb_ref.1) | copy-start | bytes 52
  7.3 50.4 %copy-start.15 = (f32[4]{0:T(128)S(1)}, f32[4]{0:T(128)}, u32[]{:S(2)}) copy-start(f32[4]{0:T(128)} %alog_ref.1) | copy-start | bytes 52
  7.3 50.4 %copy-start.16 = (f32[4]{0:T(128)S(1)}, f32[4]{0:T(128)}, u32[]{:S(2)}) copy-start(f32[4]{0:T(128)} %skip_ref.1) | copy-start | bytes 52
  57.6 6.2 %copy-start.1 = (bf16[4,256,1024]{2,1,0:T(8,128)(2,1)}, bf16[4,256,1024]{2,1,0:T(8,128)(2,1)S(1)}, u32[]{:S(2)}) copy-start(bf16[4,256,1024]{2,1,0:T(8,128)(2,1)S(1)} %get-tuple-element.26.weight_ref) | copy-start | bytes 6291460
  57.7 41.7 %copy-start.9 = (f32[256]{0:T(256)S(1)}, f32[256]{0:T(256)}, u32[]{:S(2)}) copy-start(f32[256]{0:T(256)} %param.30) | copy-start | bytes 3076
  63.8 11.4 %collective-permute-start = (f32[4,128,256]{2,1,0:T(8,128)S(1)}, f32[4,128,256]{2,1,0:T(8,128)S(1)}, u32[]{:S(2)}, u32[]{:S(2)}) collective-permute-start(f32[4,128,256]{2,1,0:T(8,128)S(1)} %get-tuple-element.22), channel_id=1, source_target_pairs={{0,4},{1,5},{2,6},{3,7},{8,12},{9,13},{10,14},{11,15},{16,20},{17,... | collective-permute-start | bytes 1572872 | tf_op jit(solution)/shard_map/ppermute | solution.py:18
  66.8 17.8 %collective-permute-start.1 = (bf16[4,256,256]{2,1,0:T(8,128)(2,1)S(1)}, bf16[4,256,256]{2,1,0:T(8,128)(2,1)S(1)}, u32[]{:S(2)}, u32[]{:S(2)}) collective-permute-start(bf16[4,256,256]{2,1,0:T(8,128)(2,1)S(1)} %get-tuple-element.24), channel_id=1, source_target_pairs={{0,8},{8,16},{16,24},{1,9},{9,17},{17,25},{2,10},{10,18},{18,26},{... | collective-permute-start | bytes 1572872 | tf_op jit(solution)/shard_map/ppermute | solution.py:18
  73.9 25.4 %collective-permute-start.2 = (bf16[4,256,256]{2,1,0:T(8,128)(2,1)S(1)}, bf16[4,256,256]{2,1,0:T(8,128)(2,1)S(1)}, u32[]{:S(2)}, u32[]{:S(2)}) collective-permute-start(bf16[4,256,256]{2,1,0:T(8,128)(2,1)S(1)} %get-tuple-element.25), channel_id=1, source_target_pairs={{8,0},{16,8},{24,16},{9,1},{17,9},{25,17},{10,2},{18,10},{26,18},{... | collective-permute-start | bytes 1572872 | tf_op jit(solution)/shard_map/ppermute | solution.py:18

commit v2 on v0

v2 whole, which is shorter than its diff:
```python
import jax
import jax.numpy as jnp
from jax import lax
from jax.experimental import pallas as pl
from jax.experimental.pallas import tpu as pltpu
from jax.sharding import PartitionSpec as P

HEAD = 64
EXTRA = 16
EPS = 1e-05
F32 = jnp.float32
BF16 = jnp.bfloat16


MESH = pl.DeviceIdType.MESH
ANY = pl.BlockSpec(memory_space=pl.ANY)
VMEM = pl.BlockSpec(memory_space=pltpu.VMEM)
SMEM = pl.BlockSpec(memory_space=pltpu.SMEM)


def slot_row(spans_ref, rank, j, count):
    start, opens, final = jnp.int32(0), jnp.int32(0), jnp.int32(0)
    for k in range(count):
        span = spans_ref[rank, k]
        inside = (j >= start) & (j < start + span)
        opens = jnp.where(inside & (j == start), 1, opens)
        final = jnp.where(inside, start + span - 1, final)
        start = start + span
    return opens == 1, final


def choose(rank_of, rank, own, left, right):
    return jnp.where(rank_of == rank, own, jnp.where(rank_of < rank, left, right))


def scan_slot(
    j, rank, source_ref, spans_ref, dtb_ref, alog_ref, skip_ref,
    own_ref, left_ref, right_ref, wx_ref, wbc_ref, bx_ref, bbc_ref,
    base_ref, scale_ref, c_ref, end_ref,
    joined, tail, state, decay, mixes, spread, weighted,
):
    count = own_ref.shape[0]
    length = own_ref.shape[1] - EXTRA
    width = wx_ref.shape[1]
    bc_width = wbc_ref.shape[1]
    states = bc_width // 2
    taps = wx_ref.shape[0]
    heads = width // HEAD
    opens, final = slot_row(spans_ref, rank, j, count)

    def moved(slot, rows):
        parts = [ref[slot, rows, :].astype(F32) for ref in (own_ref, left_ref, right_ref)]
        return choose(source_ref[rank, slot], rank, *parts)

    before = moved(final, slice(length, length + EXTRA))[EXTRA - 8 :]
    joined[0:8, :] = jnp.where(opens, before, tail[...])
    joined[8 : 8 + length, :] = moved(j, slice(0, length))
    steps = moved(j, slice(length, length + EXTRA))[0:8, :length]
    tail[...] = joined[length : length + 8, :]

    def conv(weight_ref, bias_ref, first, last):
        total = bias_ref[...]
        for k in range(taps):
            offset = 8 - (taps - 1) + k
            total = total + weight_ref[k : k + 1, :] * joined[offset : offset + length, first:last]
        return (total / (1.0 + jnp.exp(-total))).astype(BF16)

    xc = conv(wx_ref, bx_ref, 0, width)
    bc = conv(wbc_ref, bbc_ref, width, width + bc_width)
    b_rows = jnp.transpose(bc[:, :states].astype(F32))
    c_act = bc[:, states:]
    c_ref[j] = c_act

    row = lax.broadcasted_iota(jnp.int32, (8, length), 0)
    shift = jnp.zeros((8, length), F32)
    rate = jnp.zeros((8, length), F32)
    for h in range(heads):
        shift = jnp.where(row == h, dtb_ref[h], shift)
        rate = jnp.where(row == h, alog_ref[h], rate)
    raw = steps + shift
    dt = jnp.maximum(raw, 0.0) + jnp.log1p(jnp.exp(-jnp.abs(raw)))
    rates = jnp.where(row < heads, -jnp.exp(rate) * dt, 0.0)
    t_at = lax.broadcasted_iota(jnp.int32, (length, length), 0)
    s_at = lax.broadcasted_iota(jnp.int32, (length, length), 1)
    lower = t_at >= s_at
    ones = jnp.where(lower, 1.0, 0.0).astype(BF16)
    hi = rates.astype(BF16)
    mid = (rates - hi.astype(F32)).astype(BF16)
    low = (rates - hi.astype(F32) - mid.astype(F32)).astype(BF16)
    across = (((1,), (1,)), ((), ()))
    cum_rows = sum(
        lax.dot_general(part, ones, across, preferred_element_type=F32) for part in (low, mid, hi)
    )
    padded = jnp.concatenate([cum_rows] + [jnp.zeros((120, length), F32)], 0)
    cum_cols = jnp.transpose(padded)
    total = cum_rows[:, length - 1 :]
    gone = jnp.exp(total - cum_rows) * dt

    gram = jnp.dot(c_act, b_rows.astype(BF16), preferred_element_type=F32)
    lane_head = lax.broadcasted_iota(jnp.int32, (length, width), 1) // HEAD
    cum_wide = jnp.zeros((length, width), F32)
    skip_wide = jnp.zeros((1, width), F32)
    for h in range(heads):
        column = cum_cols[:, h : h + 1]
        gap = jnp.where(lower, column - cum_rows[h : h + 1, :], -jnp.inf)
        mix = gram * jnp.exp(gap) * dt[h : h + 1, :]
        mixes[:, h * length : (h + 1) * length] = mix.astype(BF16)
        weighted[:, h * length : (h + 1) * length] = (gone[h : h + 1, :] * b_rows).astype(BF16)
        spread[h * length : (h + 1) * length, :] = jnp.where(
            lane_head == h, xc.astype(F32), 0.0
        ).astype(BF16)
        cum_wide = jnp.where(lane_head == h, column, cum_wide)
        skip_wide = jnp.where(lane_head[0:1] == h, skip_ref[h], skip_wide)
    intra = jnp.dot(mixes[...], spread[...], preferred_element_type=F32)
    contrib = jnp.dot(weighted[...], spread[...], preferred_element_type=F32)

    grown = jnp.exp(cum_wide)
    block_decay = grown[length - 1 : length, :]
    entering = jnp.where(opens, 0.0, state[...])
    passed = jnp.where(opens, 1.0, decay[...])
    ent_hi = entering.astype(BF16)
    ent_lo = (entering - ent_hi.astype(F32)).astype(BF16)
    read = jnp.dot(c_act, ent_hi, preferred_element_type=F32) + jnp.dot(
        c_act, ent_lo, preferred_element_type=F32
    )
    base_ref[j] = intra + grown * read + skip_wide * xc.astype(F32)
    scale_ref[j] = grown * passed
    ended = block_decay * entering + contrib
    state[...] = ended
    decay[...] = passed * block_decay
    end_ref[j] = ended


def mixer_kernel(
    slot_ref, source_ref, spans_ref, dtb_ref, alog_ref, skip_ref,
    x_ref, z_ref, bc_ref, dt_ref, wx_ref, wbc_ref, bx_ref, bbc_ref, gain_ref, weight_in,
    out_ref,
    own_ref, left_ref, right_ref, own_gate, left_gate, right_gate, gate_send, weight_ref,
    tail_x, tail_bc, send, base_ref, scale_ref, c_ref, end_ref, carried_ref, rows,
    joined, tail, state, decay, mixes, spread, weighted,
    tail_send, tail_recv, move_send, move_recv, gate_sent, gate_came, part_send, part_recv, local,
    state_send, state_recv, right_send, left_send, arrive,
):
    ranks, pieces, groups = (lax.axis_size(axis) for axis in ("dp", "seq", "tensor"))
    d, q, m = (lax.axis_index(axis) for axis in ("dp", "seq", "tensor"))
    count = slot_ref.shape[1]
    length, width = x_ref.shape[1:]
    heads = dt_ref.shape[1]
    cols = weight_ref.shape[2]

    barrier = pltpu.get_barrier_semaphore()
    near = (
        (d > 0, {"dp": d - 1}), (d < ranks - 1, {"dp": d + 1}),
        (q > 0, {"seq": q - 1}), (q < pieces - 1, {"seq": q + 1}),
    )
    for there, target in near:
        @pl.when(there)
        def _(target=target):
            pl.semaphore_signal(barrier, inc=1, device_id=target, device_id_type=MESH)
    for k in range(1, groups):
        peer = lax.rem(m + k, groups)
        pl.semaphore_signal(barrier, inc=1, device_id={"tensor": peer}, device_id_type=MESH)
    pl.semaphore_wait(barrier, groups - 1 + sum(there.astype(jnp.int32) for there, _ in near))

    def tail_copies():
        ends = pl.ds(length - EXTRA, EXTRA)
        target = {"seq": q + 1}
        return [
            pltpu.make_async_remote_copy(
                ref.at[:, ends, :], dst, tail_send.at[i], tail_recv.at[i],
                device_id=target, device_id_type=MESH,
            )
            for i, (ref, dst) in enumerate(((x_ref, tail_x), (bc_ref, tail_bc)))
        ]

    def move(side, j):
        dst = (right_ref, left_ref)[side]
        return pltpu.make_async_remote_copy(
            send.at[side, j], dst.at[j], move_send.at[side, j], move_recv.at[side, j],
            device_id={"dp": d + (2 * side - 1)}, device_id_type=MESH,
        )

    def part(k):
        peer = lax.rem(m + k, groups)
        return pltpu.make_async_remote_copy(
            weight_in.at[:, pl.ds(pl.multiple_of(peer * cols, cols), cols)],
            weight_ref.at[m], part_send.at[k - 1], part_recv.at[k - 1],
            device_id={"tensor": peer}, device_id_type=MESH,
        )

    def arrived(k):
        peer = lax.rem(m - k + groups, groups)
        return pltpu.make_async_remote_copy(
            weight_in.at[:, pl.ds(0, cols)],
            weight_ref.at[peer], part_send.at[k - 1], part_recv.at[k - 1],
            device_id={"tensor": peer}, device_id_type=MESH,
        )

    @pl.when(q < pieces - 1)
    def _():
        for copy in tail_copies():
            copy.start()

    keep = pltpu.make_async_copy(
        weight_in.at[:, pl.ds(pl.multiple_of(m * cols, cols), cols)], weight_ref.at[m], local.at[0]
    )
    keep.start()
    for k in range(1, groups):
        part(k).start()

    @pl.when(q == 0)
    def _():
        tail_x[...] = jnp.zeros_like(tail_x)
        tail_bc[...] = jnp.zeros_like(tail_bc)

    @pl.when(q > 0)
    def _():
        for copy in tail_copies():
            copy.wait_recv()

    def fill(ref, at, slot):
        ref[at + (slice(0, length), slice(0, width))] = x_ref[slot]
        ref[at + (slice(0, length), slice(width, None))] = bc_ref[slot]
        ref[at + (slice(length, None), slice(0, width))] = tail_x[slot]
        ref[at + (slice(length, None), slice(width, None))] = tail_bc[slot]
        ref[at + (slice(length, length + heads), slice(0, length))] = dt_ref[slot]

    sides = ((d > 0, jnp.maximum(d - 1, 0)), (d < ranks - 1, jnp.minimum(d + 1, ranks - 1)))
    for j in range(count):
        for side, (there, peer) in enumerate(sides):
            fill(send, (side, j), slot_ref[peer, j])

            @pl.when(there)
            def _(side=side, j=j):
                move(side, j).start()
    for j in range(count):
        fill(own_ref, (j,), slot_ref[d, j])
        own_gate[j] = z_ref[slot_ref[d, j]]
        gate_send[0, j] = z_ref[slot_ref[sides[0][1], j]]
        gate_send[1, j] = z_ref[slot_ref[sides[1][1], j]]

    def move_gate(side):
        dst = (right_gate, left_gate)[side]
        return pltpu.make_async_remote_copy(
            gate_send.at[side], dst, gate_sent.at[side], gate_came.at[side],
            device_id={"dp": d + (2 * side - 1)}, device_id_type=MESH,
        )

    for side in range(2):
        @pl.when(sides[side][0])
        def _(side=side):
            for j in range(count):
                move(side, j).wait_send()
            move_gate(side).start()

    for side in range(2):
        @pl.when(sides[1 - side][0])
        def _(side=side):
            for j in range(count):
                move(side, j).wait_recv()

    def scan_step(j, token):
        scan_slot(
            j, d, source_ref, spans_ref, dtb_ref, alog_ref, skip_ref,
            own_ref, left_ref, right_ref, wx_ref, wbc_ref, bx_ref, bbc_ref,
            base_ref, scale_ref, c_ref, end_ref,
            joined, tail, state, decay, mixes, spread, weighted,
        )
        return token

    lax.fori_loop(0, count, scan_step, 0)

    hand = pltpu.make_async_remote_copy(
        end_ref, carried_ref, state_send.at[0], state_recv.at[0],
        device_id={"seq": q + 1}, device_id_type=MESH,
    )

    @pl.when(q < pieces - 1)
    def _():
        hand.start()

    @pl.when(q == 0)
    def _():
        carried_ref[...] = jnp.zeros_like(carried_ref)

    @pl.when(q > 0)
    def _():
        hand.wait_recv()

    for side in range(2):
        @pl.when(sides[1 - side][0])
        def _(side=side):
            move_gate(side).wait_recv()

    beside = ((m > 0, m - 1), (m < groups - 1, m + 1))

    def hop(side, source, j):
        return pltpu.make_async_remote_copy(
            rows.at[source, j], rows.at[source, j],
            (left_send, right_send)[side].at[source, j], arrive.at[source, j],
            device_id={"tensor": m + (2 * side - 1)}, device_id_type=MESH,
        )

    for j in range(count):
        _, final = slot_row(spans_ref, d, jnp.int32(j), count)
        carried = carried_ref[final]
        high = carried.astype(BF16)
        low = (carried - high.astype(F32)).astype(BF16)
        c_act = c_ref[j]
        read = jnp.dot(c_act, high, preferred_element_type=F32) + jnp.dot(
            c_act, low, preferred_element_type=F32
        )
        y = base_ref[j] + scale_ref[j] * read
        parts = [ref[j].astype(F32) for ref in (own_gate, left_gate, right_gate)]
        z = choose(source_ref[d, j], d, *parts)
        g = y * (z / (1.0 + jnp.exp(-z)))
        inverse = lax.rsqrt(jnp.mean(g * g, axis=-1, keepdims=True) + EPS)
        rows[m, j] = (g * inverse * gain_ref[...]).astype(BF16)
        for side, (there, _) in enumerate(beside):
            @pl.when(there)
            def _(side=side, j=j):
                hop(side, m, j).start()

    keep.wait()
    for k in range(1, groups):
        arrived(k).wait_recv()

    def one_slot(j, token):
        for k in range(1, groups):
            for side in range(2):
                source = m - k if side == 1 else m + k
                here = (source >= 0) if side == 1 else (source < groups)

                @pl.when(here)
                def _(side=side, source=source):
                    hop(side, source, j).wait_recv()

                @pl.when(here & beside[side][0])
                def _(side=side, source=source):
                    hop(side, source, j).start()
        total = jnp.dot(rows[0, j], weight_ref[0], preferred_element_type=F32)
        for i in range(1, groups):
            total = total + jnp.dot(rows[i, j], weight_ref[i], preferred_element_type=F32)
        out_ref[j] = total.astype(BF16)
        return token

    lax.fori_loop(0, count, one_slot, 0)

    def drain(j, token):
        for side, (there, _) in enumerate(beside):
            @pl.when(there)
            def _(side=side):
                hop(side, m, j).wait_send()
        for k in range(1, groups):
            for side in range(2):
                source = m - k if side == 1 else m + k
                here = (source >= 0) if side == 1 else (source < groups)

                @pl.when(here & beside[side][0])
                def _(side=side, source=source):
                    hop(side, source, j).wait_send()
        return token

    lax.fori_loop(0, count, drain, 0)

    for side in range(2):
        @pl.when(sides[side][0])
        def _(side=side):
            move_gate(side).wait_send()

    @pl.when(q < pieces - 1)
    def _():
        for copy in tail_copies():
            copy.wait_send()
        hand.wait_send()

    for k in range(1, groups):
        part(k).wait_send()


def body(
    entry_x, entry_z, entry_bc, entry_dt, source_rank, source_slot, row_spans,
    conv_x_weight, conv_x_bias, conv_bc_weight, conv_bc_bias,
    dt_bias, a_log, d_skip, norm_gain, out_weight,
):
    groups = lax.axis_size("tensor")
    count = source_slot.shape[1]
    slots, length, width = entry_x.shape
    bc_width = entry_bc.shape[2]
    full = width + bc_width
    heads, states = width // HEAD, bc_width // 2
    cols = out_weight.shape[1] // groups
    parts = max(groups - 1, 1)
    dma = pltpu.SemaphoreType.DMA
    main = pltpu.VMEM((count, length + EXTRA, full), BF16)
    gates = pltpu.VMEM((count, length, width), BF16)
    wide = pltpu.VMEM((count, length, width), F32)
    carry = pltpu.VMEM((count, states, width), F32)
    return pl.pallas_call(
        mixer_kernel,
        in_specs=[SMEM] * 6 + [VMEM] * 9 + [ANY],
        out_specs=VMEM,
        out_shape=jax.ShapeDtypeStruct((count, length, cols), BF16),
        scratch_shapes=[
            main, main, main, gates, gates, gates,
            pltpu.VMEM((2, count, length, width), BF16),
            pltpu.VMEM((groups, width, cols), BF16),
            pltpu.VMEM((slots, EXTRA, width), BF16),
            pltpu.VMEM((slots, EXTRA, bc_width), BF16),
            pltpu.VMEM((2, count, length + EXTRA, full), BF16),
            wide, wide, pltpu.VMEM((count, length, states), BF16), carry, carry,
            pltpu.VMEM((groups, count, length, width), BF16),
            pltpu.VMEM((length + 8, full), F32),
            pltpu.VMEM((8, full), F32),
            pltpu.VMEM((states, width), F32),
            pltpu.VMEM((1, width), F32),
            pltpu.VMEM((length, heads * length), BF16),
            pltpu.VMEM((heads * length, width), BF16),
            pltpu.VMEM((states, heads * length), BF16),
            dma((2,)), dma((2,)), dma((2, count)), dma((2, count)), dma((2,)), dma((2,)),
            dma((parts,)), dma((parts,)), dma((1,)), dma((1,)), dma((1,)),
            dma((groups, count)), dma((groups, count)), dma((groups, count)),
        ],
        compiler_params=pltpu.CompilerParams(
            collective_id=0, has_side_effects=True, vmem_limit_bytes=58 << 20
        ),
        name="mixer",
    )(
        source_slot, source_rank, row_spans, dt_bias, a_log, d_skip,
        entry_x, entry_z, entry_bc, jnp.swapaxes(entry_dt, 1, 2),
        conv_x_weight, conv_bc_weight, conv_x_bias.reshape(1, -1), conv_bc_bias.reshape(1, -1),
        norm_gain.reshape(1, -1), out_weight,
    )


def solution(mesh):
    split = P("dp", "seq", "tensor")
    placed = (
        split, split, P("dp", "seq", None), split, P(), P(), P(),
        P(None, "tensor"), P("tensor"), P(), P(),
        P("tensor"), P("tensor"), P("tensor"), P("tensor"), P("tensor", None),
    )
    return jax.shard_map(body, mesh=mesh, in_specs=placed, out_specs=split, check_vma=False)
```

time: 194 us -> 122 us (0.63)
  the two profiles are of different devices: /device:TPU:0 before, /device:TPU:4 now
where the time goes in v2:
time: 122 us
  Pallas kernels  119 us (98%)
  local copies, waits for them, and re-layouts  3.08 us (3%)
    pallas_call x1, Pallas kernels, body(): pl.pallas_call(mixer_kernel, in_specs=[SMEM] * 6 + [VMEM] * 9 + [ANY], ou...  119 us
    unnamed x1, local copies, waits for them, and re-layouts  3.08 us

profile of v2, /device:TPU:4, one launch (start us, length us, event | category | flops | bytes accessed | tf_op | source)
XLA Modules:
  0.0 122.0 jit_solution(9379717172599973269)
XLA Ops:
  0.0 118.9 %mixer.1 = bf16[4,256,1024]{2,1,0:T(8,128)(2,1)} custom-call(s32[4,4]{1,0:T(4,128)} %slot_ref.1, s32[4,4]{1,0:T(4,128)} %source_ref.1, s32[4,4]{1,0:T(4,128)} %spans_ref.1, f32[4]{0:T(128)} %dtb_ref.1, f32[4]{0:T(128)} %alog_ref.1, f32[4]{0:T(128)} %skip_ref.1, bf16[12,256,256]{2,1,0:T(8,128)(2,1)} %x_ref.1, bf16[12,256,256]{2,1,0:T(8,128)(2,1)} %z_ref.1, ...), custom_call_target="tpu_custom_call" | custom-call | tf_op jit(solution)/shard_map/mixer/pallas_call | solution.py:399
  118.9 3.1 %copy.18 = bf16[4,256,1024]{2,1,0:T(8,128)(2,1)} copy(bf16[4,256,1024]{2,1,0:T(8,128)(2,1)} %mixer.1) | data formatting | bytes 4194304

commit v3 on v2

--- a/solution.py
+++ b/solution.py
@@ -35,12 +35,13 @@
 
 def scan_slot(
     j, rank, source_ref, spans_ref, dtb_ref, alog_ref, skip_ref,
-    own_ref, left_ref, right_ref, wx_ref, wbc_ref, bx_ref, bbc_ref,
+    own_ref, left_ref, right_ref, own_ends, left_ends, right_ends,
+    wx_ref, wbc_ref, bx_ref, bbc_ref,
     base_ref, scale_ref, c_ref, end_ref,
     joined, tail, state, decay, mixes, spread, weighted,
 ):
     count = own_ref.shape[0]
-    length = own_ref.shape[1] - EXTRA
+    length = own_ref.shape[1]
     width = wx_ref.shape[1]
     bc_width = wbc_ref.shape[1]
     states = bc_width // 2
@@ -48,14 +49,14 @@
     heads = width // HEAD
     opens, final = slot_row(spans_ref, rank, j, count)
 
-    def moved(slot, rows):
-        parts = [ref[slot, rows, :].astype(F32) for ref in (own_ref, left_ref, right_ref)]
+    def moved(slot, *refs):
+        parts = [ref[slot].astype(F32) for ref in refs]
         return choose(source_ref[rank, slot], rank, *parts)
 
-    before = moved(final, slice(length, length + EXTRA))[EXTRA - 8 :]
+    before = moved(final, own_ends, left_ends, right_ends)[EXTRA - 8 :]
     joined[0:8, :] = jnp.where(opens, before, tail[...])
-    joined[8 : 8 + length, :] = moved(j, slice(0, length))
-    steps = moved(j, slice(length, length + EXTRA))[0:8, :length]
+    joined[8 : 8 + length, :] = moved(j, own_ref, left_ref, right_ref)
+    steps = moved(j, own_ends, left_ends, right_ends)[0:8, :length]
     tail[...] = joined[length : length + 8, :]
 
     def conv(weight_ref, bias_ref, first, last):
@@ -135,11 +136,12 @@
     slot_ref, source_ref, spans_ref, dtb_ref, alog_ref, skip_ref,
     x_ref, z_ref, bc_ref, dt_ref, wx_ref, wbc_ref, bx_ref, bbc_ref, gain_ref, weight_in,
     out_ref,
-    own_ref, left_ref, right_ref, own_gate, left_gate, right_gate, gate_send, weight_ref,
+    own_ref, left_ref, right_ref, own_ends, left_ends, right_ends, send_ends,
+    own_gate, left_gate, right_gate, gate_send, weight_ref,
     tail_x, tail_bc, send, base_ref, scale_ref, c_ref, end_ref, carried_ref, rows,
     joined, tail, state, decay, mixes, spread, weighted,
     tail_send, tail_recv, move_send, move_recv, gate_sent, gate_came, part_send, part_recv, local,
-    state_send, state_recv, right_send, left_send, arrive,
+    state_send, state_recv, right_send, left_send, arrive, ends_send, ends_recv,
 ):
     ranks, pieces, groups = (lax.axis_size(axis) for axis in ("dp", "seq", "tensor"))
     d, q, m = (lax.axis_index(axis) for axis in ("dp", "seq", "tensor"))
@@ -180,6 +182,13 @@
             device_id={"dp": d + (2 * side - 1)}, device_id_type=MESH,
         )
 
+    def move_ends(side):
+        dst = (right_ends, left_ends)[side]
+        return pltpu.make_async_remote_copy(
+            send_ends.at[side], dst, ends_send.at[side], ends_recv.at[side],
+            device_id={"dp": d + (2 * side - 1)}, device_id_type=MESH,
+        )
+
     def part(k):
         peer = lax.rem(m + k, groups)
         return pltpu.make_async_remote_copy(
@@ -208,6 +217,26 @@
     for k in range(1, groups):
         part(k).start()
 
+    def fill(ref, at, slot):
+        ref[at + (slice(None), slice(0, width))] = x_ref[slot]
+        ref[at + (slice(None), slice(width, None))] = bc_ref[slot]
+
+    def fill_ends(ref, at, slot):
+        ref[at + (slice(None), slice(0, width))] = tail_x[slot]
+        ref[at + (slice(None), slice(width, None))] = tail_bc[slot]
+        ref[at + (slice(0, heads), slice(0, length))] = dt_ref[slot]
+
+    sides = ((d > 0, jnp.maximum(d - 1, 0)), (d < ranks - 1, jnp.minimum(d + 1, ranks - 1)))
+    def send_slot(j):
+        for side, (there, peer) in enumerate(sides):
+            fill(send, (side, j), slot_ref[peer, j])
+
+            @pl.when(there)
+            def _(side=side):
+                move(side, j).start()
+
+    send_slot(0)
+
     @pl.when(q == 0)
     def _():
         tail_x[...] = jnp.zeros_like(tail_x)
@@ -218,51 +247,52 @@
         for copy in tail_copies():
             copy.wait_recv()
 
-    def fill(ref, at, slot):
-        ref[at + (slice(0, length), slice(0, width))] = x_ref[slot]
-        ref[at + (slice(0, length), slice(width, None))] = bc_ref[slot]
-        ref[at + (slice(length, None), slice(0, width))] = tail_x[slot]
-        ref[at + (slice(length, None), slice(width, None))] = tail_bc[slot]
-        ref[at + (slice(length, length + heads), slice(0, length))] = dt_ref[slot]
-
-    sides = ((d > 0, jnp.maximum(d - 1, 0)), (d < ranks - 1, jnp.minimum(d + 1, ranks - 1)))
-    for j in range(count):
-        for side, (there, peer) in enumerate(sides):
-            fill(send, (side, j), slot_ref[peer, j])
-
-            @pl.when(there)
-            def _(side=side, j=j):
-                move(side, j).start()
+    for side, (there, peer) in enumerate(sides):
+        for j in range(count):
+            fill_ends(send_ends, (side, j), slot_ref[peer, j])
+
+        @pl.when(there)
+        def _(side=side):
+            move_ends(side).start()
+    for j in range(1, count):
+        send_slot(j)
     for j in range(count):
         fill(own_ref, (j,), slot_ref[d, j])
+        fill_ends(own_ends, (j,), slot_ref[d, j])
         own_gate[j] = z_ref[slot_ref[d, j]]
         gate_send[0, j] = z_ref[slot_ref[sides[0][1], j]]
         gate_send[1, j] = z_ref[slot_ref[sides[1][1], j]]
 
-    def move_gate(side):
+    def move_gate(side, j):
         dst = (right_gate, left_gate)[side]
         return pltpu.make_async_remote_copy(
-            gate_send.at[side], dst, gate_sent.at[side], gate_came.at[side],
+            gate_send.at[side, j], dst.at[j], gate_sent.at[side, j], gate_came.at[side, j],
             device_id={"dp": d + (2 * side - 1)}, device_id_type=MESH,
         )
-
-    for side in range(2):
-        @pl.when(sides[side][0])
-        def _(side=side):
-            for j in range(count):
-                move(side, j).wait_send()
-            move_gate(side).start()
 
     for side in range(2):
         @pl.when(sides[1 - side][0])
         def _(side=side):
-            for j in range(count):
+            move_ends(side).wait_recv()
+
+    def scan_step(j, token):
+        for side in range(2):
+            @pl.when(sides[1 - side][0])
+            def _(side=side):
                 move(side, j).wait_recv()
 
-    def scan_step(j, token):
+        for side in range(2):
+            @pl.when(sides[side][0] & (j == count - 1))
+            def _(side=side):
+                for i in range(count):
+                    move(side, i).wait_send()
+                for i in range(count):
+                    move_gate(side, i).start()
+
         scan_slot(
             j, d, source_ref, spans_ref, dtb_ref, alog_ref, skip_ref,
-            own_ref, left_ref, right_ref, wx_ref, wbc_ref, bx_ref, bbc_ref,
+            own_ref, left_ref, right_ref, own_ends, left_ends, right_ends,
+            wx_ref, wbc_ref, bx_ref, bbc_ref,
             base_ref, scale_ref, c_ref, end_ref,
             joined, tail, state, decay, mixes, spread, weighted,
         )
@@ -287,11 +317,6 @@
     def _():
         hand.wait_recv()
 
-    for side in range(2):
-        @pl.when(sides[1 - side][0])
-        def _(side=side):
-            move_gate(side).wait_recv()
-
     beside = ((m > 0, m - 1), (m < groups - 1, m + 1))
 
     def hop(side, source, j):
@@ -301,8 +326,13 @@
             device_id={"tensor": m + (2 * side - 1)}, device_id_type=MESH,
         )
 
-    for j in range(count):
-        _, final = slot_row(spans_ref, d, jnp.int32(j), count)
+    def gate_slot(j):
+        for side in range(2):
+            @pl.when(sides[1 - side][0])
+            def _(side=side):
+                move_gate(side, j).wait_recv()
+
+        _, final = slot_row(spans_ref, d, j, count)
         carried = carried_ref[final]
         high = carried.astype(BF16)
         low = (carried - high.astype(F32)).astype(BF16)
@@ -318,14 +348,14 @@
         rows[m, j] = (g * inverse * gain_ref[...]).astype(BF16)
         for side, (there, _) in enumerate(beside):
             @pl.when(there)
-            def _(side=side, j=j):
+            def _(side=side):
                 hop(side, m, j).start()
 
     keep.wait()
     for k in range(1, groups):
         arrived(k).wait_recv()
 
-    def one_slot(j, token):
+    def project_slot(j):
         for k in range(1, groups):
             for side in range(2):
                 source = m - k if side == 1 else m + k
@@ -342,9 +372,19 @@
         for i in range(1, groups):
             total = total + jnp.dot(rows[i, j], weight_ref[i], preferred_element_type=F32)
         out_ref[j] = total.astype(BF16)
+
+    def turn(j, token):
+        @pl.when(j < count)
+        def _():
+            gate_slot(j)
+
+        @pl.when(j > 0)
+        def _():
+            project_slot(j - 1)
+
         return token
 
-    lax.fori_loop(0, count, one_slot, 0)
+    lax.fori_loop(0, count + 1, turn, 0)
 
     def drain(j, token):
         for side, (there, _) in enumerate(beside):
@@ -366,7 +406,9 @@
     for side in range(2):
         @pl.when(sides[side][0])
         def _(side=side):
-            move_gate(side).wait_send()
+            move_ends(side).wait_send()
+            for j in range(count):
+                move_gate(side, j).wait_send()
 
     @pl.when(q < pieces - 1)
     def _():
@@ -392,7 +434,8 @@
     cols = out_weight.shape[1] // groups
     parts = max(groups - 1, 1)
     dma = pltpu.SemaphoreType.DMA
-    main = pltpu.VMEM((count, length + EXTRA, full), BF16)
+    main = pltpu.VMEM((count, length, full), BF16)
+    ends = pltpu.VMEM((count, EXTRA, full), BF16)
     gates = pltpu.VMEM((count, length, width), BF16)
     wide = pltpu.VMEM((count, length, width), F32)
     carry = pltpu.VMEM((count, states, width), F32)
@@ -402,12 +445,13 @@
         out_specs=VMEM,
         out_shape=jax.ShapeDtypeStruct((count, length, cols), BF16),
         scratch_shapes=[
-            main, main, main, gates, gates, gates,
+            main, main, main, ends, ends, ends, pltpu.VMEM((2, count, EXTRA, full), BF16),
+            gates, gates, gates,
             pltpu.VMEM((2, count, length, width), BF16),
             pltpu.VMEM((groups, width, cols), BF16),
             pltpu.VMEM((slots, EXTRA, width), BF16),
             pltpu.VMEM((slots, EXTRA, bc_width), BF16),
-            pltpu.VMEM((2, count, length + EXTRA, full), BF16),
+            pltpu.VMEM((2, count, length, full), BF16),
             wide, wide, pltpu.VMEM((count, length, states), BF16), carry, carry,
             pltpu.VMEM((groups, count, length, width), BF16),
             pltpu.VMEM((length + 8, full), F32),
@@ -417,9 +461,9 @@
             pltpu.VMEM((length, heads * length), BF16),
             pltpu.VMEM((heads * length, width), BF16),
             pltpu.VMEM((states, heads * length), BF16),
-            dma((2,)), dma((2,)), dma((2, count)), dma((2, count)), dma((2,)), dma((2,)),
-            dma((parts,)), dma((parts,)), dma((1,)), dma((1,)), dma((1,)),
-            dma((groups, count)), dma((groups, count)), dma((groups, count)),
+            dma((2,)), dma((2,)), dma((2, count)), dma((2, count)),
+            dma((2, count)), dma((2, count)), dma((parts,)), dma((parts,)), dma((1,)), dma((1,)), dma((1,)),
+            dma((groups, count)), dma((groups, count)), dma((groups, count)), dma((2,)), dma((2,)),
         ],
         compiler_params=pltpu.CompilerParams(
             collective_id=0, has_side_effects=True, vmem_limit_bytes=58 << 20

time: 122 us -> 116 us (0.951)
  the two profiles are of different devices: /device:TPU:4 before, /device:TPU:6 now
where the time goes in v3:
time: 116 us
  Pallas kernels  113 us (97%)
  local copies, waits for them, and re-layouts  3.08 us (3%)
    pallas_call x1, Pallas kernels, body(): pl.pallas_call(mixer_kernel, in_specs=[SMEM] * 6 + [VMEM] * 9 + [ANY], ou...  113 us
    unnamed x1, local copies, waits for them, and re-layouts  3.08 us

profile of v3, /device:TPU:6, one launch (start us, length us, event | category | flops | bytes accessed | tf_op | source)
XLA Modules:
  0.0 115.7 jit_solution(435867813830392309)
XLA Ops:
  0.0 112.6 %mixer.1 = bf16[4,256,1024]{2,1,0:T(8,128)(2,1)} custom-call(s32[4,4]{1,0:T(4,128)} %slot_ref.1, s32[4,4]{1,0:T(4,128)} %source_ref.1, s32[4,4]{1,0:T(4,128)} %spans_ref.1, f32[4]{0:T(128)} %dtb_ref.1, f32[4]{0:T(128)} %alog_ref.1, f32[4]{0:T(128)} %skip_ref.1, bf16[12,256,256]{2,1,0:T(8,128)(2,1)} %x_ref.1, bf16[12,256,256]{2,1,0:T(8,128)(2,1)} %z_ref.1, ...), custom_call_target="tpu_custom_call" | custom-call | tf_op jit(solution)/shard_map/mixer/pallas_call | solution.py:442
  112.7 3.1 %copy.18 = bf16[4,256,1024]{2,1,0:T(8,128)(2,1)} copy(bf16[4,256,1024]{2,1,0:T(8,128)(2,1)} %mixer.1) | data formatting | bytes 4194304
